TPU v7x, 256 devices: a whole 4x4x8 slice. The times are simulated.
256 devices in a mesh: row: 16 (over y, z_hi, core), col: 16 (over z_lo, x).
Axes of the slice: x: 4, y: 4, z: 8 (z_hi: 2, z_lo: 4; z = z_hi * 4 + z_lo), core: 2. Of those that a mesh axis runs over, the one named last changes fastest.
Arguments:
- object_field: float32 [2, 4096, 4096], P(None, 'row', 'col'), may hold values from -4 to 4
- modes: bfloat16 [16, 12, 2, 256, 256], P('row', None, None, 'col'), may hold values from -5 to 5
- coeffs: float32 [16, 16, 4, 12], P('row', 'col'), may hold values from -1.5 to 1.5
- offsets: int32 [16, 16, 4, 2], P('row', 'col'), may hold values from -128 to 128, as said below
- region: int32 [16, 16, 4], P('row', 'col'), may hold values from 0 to 15, as said below
- counts: int32 [16, 16], P('row', 'col'), may hold values from 1 to 4, as said below
- intensity: bfloat16 [16, 16, 4, 256, 256], P('row', 'col'), may hold values from 0.049804688 to 4
Outputs:
- object_grad: float32 [2, 4096, 4096], P(None, 'row', 'col')
- mode_grad: float32 [16, 12, 2, 256, 256], P('row', None, None, 'col')
Inputs may be any that keep to these rules, and one draw needn't show every extreme that they name: `offsets`: every window reaches at most 128 cells beyond its tile on each side; every tile has a live slot whose window starts at row offset -128 and column offset 256 - 256 / 2. A position's region is its tile's row index or the next one; slot 0 of every tile has its own row's region. Slots 0 to counts - 1 of a tile are live, the rest are ignored; some tile is full and some tile has one live slot.
All inputs are finite; a program needn't handle non-finite values.
Results may differ from a plain program's by a relative error of at most 0.014.
Values may be sent and summed in bfloat16 or wider, within the bound.
A program may use at most 64 MiB of HBM per device.

v0:
```python
import math

import jax
import jax.numpy as jnp
from jax import lax
from jax.sharding import PartitionSpec as P

FLOOR = 0.25


def extended_2(x, sides, width):
    for axis, dim in sides:
        size, length = (lax.axis_size(axis), x.shape[dim])
        up = [(i, (i + 1) % size) for i in range(size - 1)]
        down = [(j, i) for i, j in up]
        last = lax.slice_in_dim(x, length - width, length, axis=dim)
        leading = lax.slice_in_dim(x, 0, width, axis=dim)
        before = lax.ppermute(last, axis, up)
        after = lax.ppermute(leading, axis, down)
        x = jnp.concatenate([before, x, after], axis=dim)
    return x


def from_behind(value, axis, steps):
    count = lax.axis_size(axis)
    leading, last = (max(0, -steps), min(count, count - steps))
    return lax.ppermute(value, axis, [(source, source + steps) for source in range(leading, last)])


def dft_tables(length):
    indices = jnp.arange(length, dtype=jnp.int32)
    phases = indices[:, None] * indices[None, :] % length
    angles = phases.astype(jnp.float32) * (2.0 * math.pi / length)
    scaling = 1.0 / math.sqrt(length)
    return (
        (jnp.cos(angles) * scaling).astype(jnp.bfloat16),
        (-jnp.sin(angles) * scaling).astype(jnp.bfloat16),
    )


def left_apply(table_re, table_im, real_part, imag_part, orient):

    def multiply(table, operand):
        return jnp.einsum("mr,prn->pmn", table, operand, preferred_element_type=jnp.float32)

    out_re = multiply(table_re, real_part) - orient * multiply(table_im, imag_part)
    out_im = multiply(table_re, imag_part) + orient * multiply(table_im, real_part)
    return (out_re, out_im)


def right_apply(table_re, table_im, real_part, imag_part, orient):

    def multiply(operand, table):
        return jnp.einsum("pmc,cn->pmn", operand, table, preferred_element_type=jnp.float32)

    out_re = multiply(real_part, table_re) - orient * multiply(imag_part, table_im)
    out_im = multiply(imag_part, table_re) + orient * multiply(real_part, table_im)
    return (out_re, out_im)


def local(object_field, modes, coeffs, offsets, region, counts, intensity):
    window_size = modes.shape[-1]
    half_size = window_size // 2
    num_modes = modes.shape[1]
    slot_count = coeffs.shape[2]
    row_index = lax.axis_index("row")
    object_low = object_field.astype(jnp.bfloat16)
    extended = extended_2(object_low, (("row", 1), ("col", 2)), half_size)
    follower = from_behind(modes, "row", -1)
    stacked = jnp.concatenate([modes[0], follower[0]], axis=0)
    stack_count = stacked.shape[0]
    weights = coeffs[0, 0]
    regions = region[0, 0]
    own_mask = (regions == row_index).astype(jnp.float32)
    next_mask = (regions == row_index + 1).astype(jnp.float32)
    mixing = jnp.concatenate([weights * own_mask[:, None], weights * next_mask[:, None]], axis=1)
    portion = lax.all_gather(stacked, "col", axis=2, tiled=True)
    flattened = portion.reshape(portion.shape[0], -1).astype(jnp.float32)
    probe_part = jnp.dot(
        mixing, flattened, precision=lax.Precision.HIGHEST, preferred_element_type=jnp.float32
    )
    probes = probe_part.reshape(slot_count, 2, portion.shape[2], portion.shape[3]).astype(
        jnp.bfloat16
    )
    corners = offsets[0, 0]

    def cut_window(corner):
        return lax.dynamic_slice(
            extended,
            (jnp.int32(0), corner[0] + half_size, corner[1] + half_size),
            (2, window_size, window_size),
        )

    windows = jax.vmap(cut_window)(corners)
    probe_re = probes[:, 0].astype(jnp.float32)
    probe_im = probes[:, 1].astype(jnp.float32)
    window_re = windows[:, 0].astype(jnp.float32)
    window_im = windows[:, 1].astype(jnp.float32)
    exit_re = (probe_re * window_re - probe_im * window_im).astype(jnp.bfloat16)
    exit_im = (probe_re * window_im + probe_im * window_re).astype(jnp.bfloat16)
    table_re, table_im = dft_tables(window_size)
    half_re, half_im = left_apply(table_re, table_im, exit_re, exit_im, 1.0)
    far_re, far_im = right_apply(
        table_re, table_im, half_re.astype(jnp.bfloat16), half_im.astype(jnp.bfloat16), 1.0
    )
    magnitude = jnp.sqrt(far_re * far_re + far_im * far_im)
    measured = jnp.sqrt(intensity[0, 0].astype(jnp.float32))
    live = (jnp.arange(slot_count, dtype=jnp.int32) < counts[0, 0]).astype(jnp.float32)
    factor = (measured / jnp.maximum(magnitude, FLOOR) - 1.0) * live[:, None, None]
    change_re = (far_re * factor).astype(jnp.bfloat16)
    change_im = (far_im * factor).astype(jnp.bfloat16)
    back_re, back_im = left_apply(table_re, table_im, change_re, change_im, -1.0)
    update_re, update_im = right_apply(
        table_re, table_im, back_re.astype(jnp.bfloat16), back_im.astype(jnp.bfloat16), -1.0
    )
    object_terms = jnp.stack(
        [probe_re * update_re + probe_im * update_im, probe_re * update_im - probe_im * update_re],
        axis=1,
    )
    terms = jnp.stack(
        [
            window_re * update_re + window_im * update_im,
            window_re * update_im - window_im * update_re,
        ],
        axis=1,
    ).astype(jnp.bfloat16)

    def place(position, accum):
        start_row = corners[position, 0] + half_size
        start_col = corners[position, 1] + half_size
        current = lax.dynamic_slice(
            accum, (jnp.int32(0), start_row, start_col), (2, window_size, window_size)
        )
        return lax.dynamic_update_slice(
            accum, current + object_terms[position], (jnp.int32(0), start_row, start_col)
        )

    accum = lax.fori_loop(0, slot_count, place, jnp.zeros(extended.shape, jnp.float32))
    partial_sum = jnp.dot(
        mixing.T,
        terms.reshape(slot_count, -1).astype(jnp.float32),
        precision=lax.Precision.HIGHEST,
        preferred_element_type=jnp.float32,
    )
    partial_sum = partial_sum.reshape(stack_count, 2, window_size, window_size)
    summed = lax.psum_scatter(
        partial_sum.astype(jnp.bfloat16), "col", scatter_dimension=2, tiled=True
    ).astype(jnp.float32)
    own_sum = summed[:num_modes]
    passed = from_behind(summed[num_modes:].astype(jnp.bfloat16), "row", 1).astype(jnp.float32)
    mode_grad = (own_sum + passed)[None]
    outer_rows = jnp.concatenate([accum[:, :half_size], accum[:, -half_size:]], axis=1)
    got_rows = extended_2(outer_rows.astype(jnp.bfloat16), (("row", 1),), half_size).astype(
        outer_rows.dtype
    )
    middle = accum[:, half_size:-half_size]
    middle = middle.at[:, :half_size].add(got_rows[:, :half_size])
    middle = middle.at[:, -half_size:].add(got_rows[:, -half_size:])
    outer_cols = jnp.concatenate([middle[:, :, :half_size], middle[:, :, -half_size:]], axis=2)
    got_cols = extended_2(outer_cols.astype(jnp.bfloat16), (("col", 2),), half_size).astype(
        outer_cols.dtype
    )
    object_grad = middle[:, :, half_size:-half_size]
    object_grad = object_grad.at[:, :, :half_size].add(got_cols[:, :, :half_size])
    object_grad = object_grad.at[:, :, -half_size:].add(got_cols[:, :, -half_size:])
    return (object_grad, mode_grad)


def solution(mesh):
    in_specs = (
        P(None, "row", "col"),
        P("row", None, None, "col", None),
        P("row", "col", None, None),
        P("row", "col", None, None),
        P("row", "col", None),
        P("row", "col"),
        P("row", "col", None, None, None),
    )
    out_specs = (P(None, "row", "col"), P("row", None, None, "col", None))
    return jax.shard_map(local, mesh=mesh, in_specs=in_specs, out_specs=out_specs, check_vma=False)
```

profile of v0, /device:TPU:16, one launch (start us, length us, event | category | flops | bytes accessed | tf_op | source)
XLA Modules:
  0.0 292.4 jit_solution(9769774042760329141)
XLA Ops:
  7.2 8.4 %collective-permute-start = (bf16[1,12,2,16,256]{4,3,2,1,0:T(8,128)(2,1)}, bf16[1,12,2,16,256]{4,3,2,1,0:T(8,128)(2,1)S(1)}, u32[]{:S(2)}, u32[]{:S(2)}) collective-permute-start(bf16[1,12,2,16,256]{4,3,2,1,0:T(8,128)(2,1)} %param.18), channel_id=1, source_target_pairs={{16,0},{32,16},{48,32},{64,48},{80,64},{96,80},{112,96},{128,112},... | collective-permute-start | bytes 589832 | tf_op jit(solution)/shard_map/ppermute | solution.py:27
  15.7 3.7 %collective-permute-done = bf16[1,12,2,16,256]{4,3,2,1,0:T(8,128)(2,1)S(1)} collective-permute-done((bf16[1,12,2,16,256]{4,3,2,1,0:T(8,128)(2,1)}, bf16[1,12,2,16,256]{4,3,2,1,0:T(8,128)(2,1)S(1)}, u32[]{:S(2)}, u32[]{:S(2)}) %collective-permute-start) | collective-permute-done | bytes 196640 | tf_op jit(solution)/shard_map/ppermute | solution.py:27
  19.4 1.7 pad_maximum_fusion.4
  22.2 2.6 collective-permute-start.1
  24.9 7.9 %collective-permute-start.2 = (bf16[2,128,256]{2,1,0:T(8,128)(2,1)S(1)}, bf16[2,128,256]{2,1,0:T(8,128)(2,1)S(1)}, u32[]{:S(2)}, u32[]{:S(2)}) collective-permute-start(bf16[2,128,256]{2,1,0:T(8,128)(2,1)S(1)} %get-tuple-element.272), channel_id=1, source_target_pairs={{16,0},{32,16},{48,32},{64,48},{80,64},{96,80},{112,96},{128,112},... | collective-permute-start | bytes 393224 | tf_op jit(solution)/shard_map/ppermute | solution.py:19
  33.5 1.6 collective-permute-done.1
  35.4 3.4 %collective-permute-start.3 = (bf16[2,512,128]{2,1,0:T(8,128)(2,1)S(1)}, bf16[2,512,128]{2,1,0:T(8,128)(2,1)S(1)}, u32[]{:S(2)}, u32[]{:S(2)}) collective-permute-start(bf16[2,512,128]{2,1,0:T(8,128)(2,1)S(1)} %get-tuple-element.267), channel_id=1, source_target_pairs={{0,1},{1,2},{2,3},{3,4},{4,5},{5,6},{6,7},{7,8},{8,9},{9,10},{10,1... | collective-permute-start | bytes 786440 | tf_op jit(solution)/shard_map/ppermute | solution.py:18
  38.9 1.3 collective-permute-start.4
  40.3 7.4 %collective-permute-done.3 = bf16[2,512,128]{2,1,0:T(8,128)(2,1)S(1)} collective-permute-done((bf16[2,512,128]{2,1,0:T(8,128)(2,1)S(1)}, bf16[2,512,128]{2,1,0:T(8,128)(2,1)S(1)}, u32[]{:S(2)}, u32[]{:S(2)}) %collective-permute-start.3) | collective-permute-done | bytes 262176 | tf_op jit(solution)/shard_map/ppermute | solution.py:18
  47.7 6.4 %collective-permute-done.4 = bf16[2,512,128]{2,1,0:T(8,128)(2,1)S(1)} collective-permute-done((bf16[2,512,128]{2,1,0:T(8,128)(2,1)S(1)}, bf16[2,512,128]{2,1,0:T(8,128)(2,1)S(1)}, u32[]{:S(2)}, u32[]{:S(2)}) %collective-permute-start.4) | collective-permute-done | bytes 262176 | tf_op jit(solution)/shard_map/ppermute | solution.py:19
  54.3 8.4 %while.22 = (s32[]{:T(128)}, bf16[2,512,512]{2,1,0:T(8,128)(2,1)S(1)}, s32[4,3]{1,0:T(4,128)S(1)}, bf16[4,2,256,256]{3,2,0,1:T(8,128)(2,1)S(1)}, s32[]{:T(128)}) while((s32[]{:T(128)}, bf16[2,512,512]{2,1,0:T(8,128)(2,1)S(1)}, s32[4,3]{1,0:T(4,128)S(1)}, bf16[4,2,256,256]{3,2,0,1:T(8,128)(2,1)S(1)}, s32[]{:T(128)}) %tuple.105), condition=%wide.while_cond.4, body=%wide.while_body.4.sunk | while | flops 2 | bytes 524413 | solution.py:88
  54.9 1.4 bitcast_dynamic-update-slice_fusion.2
  57.0 1.4 bitcast_dynamic-update-slice_fusion.2
  59.1 1.4 bitcast_dynamic-update-slice_fusion.2
  61.2 1.4 bitcast_dynamic-update-slice_fusion.2
  62.7 58.2 %all-gather.2.cloned.1.call-done = bf16[24,2,256,256]{3,2,1,0:T(8,128)(2,1)} async-done(((bf16[24,2,16,256]{3,2,1,0:T(8,128)(2,1)}), bf16[24,2,256,256]{3,2,1,0:T(8,128)(2,1)}) %all-gather.2.cloned.1.call-update) | async-done | bytes 6291472 | tf_op jit(solution)/shard_map/all_gather | solution.py:77
  120.9 9.8 %fusion = bf16[4,2,256,256]{3,0,2,1:T(4,128)(2,1)S(1)} fusion(bf16[2,256,256,24]{2,1,0,3:T(8,128)(2,1)} %bitcast.184, f32[4,12]{1,0:T(4,128)S(1)} %get-tuple-element.274, f32[4,12]{1,0:T(4,128)S(1)} %get-tuple-element.273), kind=kOutput, calls=%fused_computation.5 | convolution fusion | flops 150995040 | bytes 7340416 | tf_op jit(solution)/shard_map/dot_general | solution.py:79
  135.0 1.3 fusion.10
  138.8 1.3 convolution_add_fusion
  140.1 2.0 multiply_convert_fusion.1
  142.1 1.5 fusion.56
  146.1 1.3 fusion.12
  148.6 1.3 fusion.54
  149.9 1.3 fusion.2
  151.1 1.8 fusion.29
  153.9 6.1 %convolution_convert_fusion = bf16[24,2,256,256]{3,0,2,1:T(8,128)(2,1)S(1)} fusion(bf16[2,256,256,4]{2,3,1,0:T(4,128)(2,1)S(1)} %bitcast.183, f32[4,12]{1,0:T(4,128)S(1)} %get-tuple-element.274, f32[4,12]{1,0:T(4,128)S(1)} %get-tuple-element.273), kind=kOutput, calls=%fused_computation.7 | convolution fusion | flops 154140768 | bytes 7340416 | tf_op jit(solution)/shard_map/dot_general | solution.py:139
  160.6 5.5 %copy.187 = bf16[32,8,48,256]{3,1,2,0:T(8,128)(2,1)} copy(bf16[32,8,48,256]{3,2,1,0:T(8,128)(2,1)S(1)} %bitcast.182) | data formatting | bytes 12582912
  166.1 1.6 pad_maximum_fusion
  168.0 48.6 %while.21 = (s32[]{:T(128)}, f32[2,512,512]{2,1,0:T(8,128)S(1)}, s32[4,2]{0,1:T(2,128)S(1)}, f32[4,2,256,256]{3,2,0,1:T(8,128)}, s32[]{:T(128)}, /*index=5*/s32[1,1]{0,1:T(1,128)}, s32[]{:T(128)}, s32[1,1]{0,1:T(1,128)}) while((s32[]{:T(128)}, f32[2,512,512]{2,1,0:T(8,128)S(1)}, s32[4,2]{0,1:T(2,128)S(1)}, f32[4,2,256,256]{3,2,0,1:T(8,128)}, ...), condition=%wide.region_1.2_spmd, body=%wide.region_0.1_spmd.sunk | while | flops 131082 | bytes 2621661 | solution.py:138
  171.0 1.3 bitcast_add_fusion.2
  172.3 8.9 %dynamic_update_slice.12 = f32[2,512,512]{2,1,0:T(8,128)S(1)} dynamic-update-slice(f32[2,512,512]{2,1,0:T(8,128)S(1)} %get-tuple-element.361, f32[2,256,256]{2,1,0:T(8,128)S(1)} %bitcast_add_fusion.2, s32[]{:T(128)} %constant.197.clone.1..sunk, s32[]{:T(128)S(6)} %select_n.116, s32[]{:T(128)S(6)} %select_n.117) | dynamic-update-slice | bytes 1048580 | tf_op jit(solution)/shard_map/while/body/eval_jaxpr/dynamic_update_slice | solution.py:134
  184.3 1.3 bitcast_add_fusion.2
  185.5 8.1 %dynamic_update_slice.12 = f32[2,512,512]{2,1,0:T(8,128)S(1)} dynamic-update-slice(f32[2,512,512]{2,1,0:T(8,128)S(1)} %get-tuple-element.361, f32[2,256,256]{2,1,0:T(8,128)S(1)} %bitcast_add_fusion.2, s32[]{:T(128)} %constant.197.clone.1..sunk, s32[]{:T(128)S(6)} %select_n.116, s32[]{:T(128)S(6)} %select_n.117) | dynamic-update-slice | bytes 1048580 | tf_op jit(solution)/shard_map/while/body/eval_jaxpr/dynamic_update_slice | solution.py:134
  196.7 1.3 bitcast_add_fusion.2
  198.0 6.0 %dynamic_update_slice.12 = f32[2,512,512]{2,1,0:T(8,128)S(1)} dynamic-update-slice(f32[2,512,512]{2,1,0:T(8,128)S(1)} %get-tuple-element.361, f32[2,256,256]{2,1,0:T(8,128)S(1)} %bitcast_add_fusion.2, s32[]{:T(128)} %constant.197.clone.1..sunk, s32[]{:T(128)S(6)} %select_n.116, s32[]{:T(128)S(6)} %select_n.117) | dynamic-update-slice | bytes 1048580 | tf_op jit(solution)/shard_map/while/body/eval_jaxpr/dynamic_update_slice | solution.py:134
  207.1 1.3 bitcast_add_fusion.2
  208.4 8.2 %dynamic_update_slice.12 = f32[2,512,512]{2,1,0:T(8,128)S(1)} dynamic-update-slice(f32[2,512,512]{2,1,0:T(8,128)S(1)} %get-tuple-element.361, f32[2,256,256]{2,1,0:T(8,128)S(1)} %bitcast_add_fusion.2, s32[]{:T(128)} %constant.197.clone.1..sunk, s32[]{:T(128)S(6)} %select_n.116, s32[]{:T(128)S(6)} %select_n.117) | dynamic-update-slice | bytes 1048580 | tf_op jit(solution)/shard_map/while/body/eval_jaxpr/dynamic_update_slice | solution.py:134
  216.8 1.9 collective-permute-start.5
  218.7 8.4 %collective-permute-start.6 = (bf16[2,128,512]{2,1,0:T(8,128)(2,1)S(1)}, bf16[2,128,512]{2,1,0:T(8,128)(2,1)S(1)}, u32[]{:S(2)}, u32[]{:S(2)}) collective-permute-start(bf16[2,128,512]{2,1,0:T(8,128)(2,1)S(1)} %get-tuple-element.264), channel_id=1, source_target_pairs={{16,0},{32,16},{48,32},{64,48},{80,64},{96,80},{112,96},{128,112},... | collective-permute-start | bytes 786440 | tf_op jit(solution)/shard_map/ppermute | solution.py:19
  227.2 11.7 %collective-permute-done.5 = bf16[2,128,512]{2,1,0:T(8,128)(2,1)S(1)} collective-permute-done((bf16[2,128,512]{2,1,0:T(8,128)(2,1)S(1)}, bf16[2,128,512]{2,1,0:T(8,128)(2,1)S(1)}, u32[]{:S(2)}, u32[]{:S(2)}) %collective-permute-start.5) | collective-permute-done | bytes 262176 | tf_op jit(solution)/shard_map/ppermute | solution.py:18
  238.9 1.4 collective-permute-done.6
  240.6 1.3 collective-permute-start.7
  241.9 1.3 collective-permute-start.8
  243.3 4.3 %collective-permute-done.7 = bf16[2,256,128]{2,1,0:T(8,128)(2,1)S(1)} collective-permute-done((bf16[2,256,128]{2,1,0:T(8,128)(2,1)S(1)}, bf16[2,256,128]{2,1,0:T(8,128)(2,1)S(1)}, u32[]{:S(2)}, u32[]{:S(2)}) %collective-permute-start.7) | collective-permute-done | bytes 131104 | tf_op jit(solution)/shard_map/ppermute | solution.py:18
  247.5 2.2 collective-permute-done.8
  249.8 20.6 %reduce-scatter.5.cloned.1.call-done = bf16[16,12288]{1,0:T(8,128)(2,1)} async-done(((bf16[256,12288]{1,0:T(8,128)(2,1)}), bf16[16,12288]{1,0:T(8,128)(2,1)}) %reduce-scatter.5.cloned.1.call-update) | async-done | bytes 393232
  271.6 1.9 collective-permute-start.9
  273.6 10.5 %collective-permute-done.9 = bf16[12,2,16,256]{3,0,2,1:T(8,128)(2,1)S(1)} collective-permute-done((bf16[12,2,16,256]{3,0,2,1:T(8,128)(2,1)S(1)}, bf16[12,2,16,256]{3,0,2,1:T(8,128)(2,1)S(1)}, u32[]{:S(2)}, u32[]{:S(2)}) %collective-permute-start.9) | collective-permute-done | bytes 196640 | tf_op jit(solution)/shard_map/ppermute | solution.py:27
  (70 shorter events, 22.0 us)
Async XLA Ops:
  7.2 25.6 %copy-start.1 = (s32[1,1,4,2]{2,3,1,0:T(2,128)S(1)}, s32[1,1,4,2]{2,3,1,0:T(2,128)}, u32[]{:S(2)}) copy-start(s32[1,1,4,2]{2,3,1,0:T(2,128)} %param.20) | copy-start | bytes 100
  7.2 25.7 %copy-start.3 = (s32[1,1,4]{2,1,0:T(1,128)S(1)}, s32[1,1,4]{2,1,0:T(1,128)}, u32[]{:S(2)}) copy-start(s32[1,1,4]{2,1,0:T(1,128)} %param.21) | copy-start | bytes 52
  7.2 113.7 %all-gather.2.cloned.1.call-start = ((), (), s32[]{:S(2)}) async-start(), calls=%async_computation.1 | async-start | bytes 6684672 | tf_op jit(solution)/shard_map/all_gather | solution.py:77
  7.2 12.1 %collective-permute-start = (bf16[1,12,2,16,256]{4,3,2,1,0:T(8,128)(2,1)}, bf16[1,12,2,16,256]{4,3,2,1,0:T(8,128)(2,1)S(1)}, u32[]{:S(2)}, u32[]{:S(2)}) collective-permute-start(bf16[1,12,2,16,256]{4,3,2,1,0:T(8,128)(2,1)} %param.18), channel_id=1, source_target_pairs={{16,0},{32,16},{48,32},{64,48},{80,64},{96,80},{112,96},{128,112},... | collective-permute-start | bytes 589832 | tf_op jit(solution)/shard_map/ppermute | solution.py:27
  21.1 19.2 %copy-start.2 = (f32[1,1,4,12]{3,2,1,0:T(4,128)S(1)}, f32[1,1,4,12]{3,2,1,0:T(4,128)}, u32[]{:S(2)}) copy-start(f32[1,1,4,12]{3,2,1,0:T(4,128)} %param.19) | copy-start | bytes 580
  21.1 249.3 %reduce-scatter.5.cloned.1.call-start = ((), (), s32[]{:S(2)}) async-start(), calls=%async_computation.2 | async-start | bytes 6684672
  22.2 12.9 %collective-permute-start.1 = (bf16[2,128,256]{2,1,0:T(8,128)(2,1)S(1)}, bf16[2,128,256]{2,1,0:T(8,128)(2,1)S(1)}, u32[]{:S(2)}, u32[]{:S(2)}) collective-permute-start(bf16[2,128,256]{2,1,0:T(8,128)(2,1)S(1)} %get-tuple-element.271), channel_id=1, source_target_pairs={{0,16},{16,32},{32,48},{48,64},{64,80},{80,96},{96,112},{112,128},... | collective-permute-start | bytes 393224 | tf_op jit(solution)/shard_map/ppermute | solution.py:18
  24.9 10.4 %collective-permute-start.2 = (bf16[2,128,256]{2,1,0:T(8,128)(2,1)S(1)}, bf16[2,128,256]{2,1,0:T(8,128)(2,1)S(1)}, u32[]{:S(2)}, u32[]{:S(2)}) collective-permute-start(bf16[2,128,256]{2,1,0:T(8,128)(2,1)S(1)} %get-tuple-element.272), channel_id=1, source_target_pairs={{16,0},{32,16},{48,32},{64,48},{80,64},{96,80},{112,96},{128,112},... | collective-permute-start | bytes 393224 | tf_op jit(solution)/shard_map/ppermute | solution.py:19
  35.4 12.3 %collective-permute-start.3 = (bf16[2,512,128]{2,1,0:T(8,128)(2,1)S(1)}, bf16[2,512,128]{2,1,0:T(8,128)(2,1)S(1)}, u32[]{:S(2)}, u32[]{:S(2)}) collective-permute-start(bf16[2,512,128]{2,1,0:T(8,128)(2,1)S(1)} %get-tuple-element.267), channel_id=1, source_target_pairs={{0,1},{1,2},{2,3},{3,4},{4,5},{5,6},{6,7},{7,8},{8,9},{9,10},{10,1... | collective-permute-start | bytes 786440 | tf_op jit(solution)/shard_map/ppermute | solution.py:18
  38.9 15.3 %collective-permute-start.4 = (bf16[2,512,128]{2,1,0:T(8,128)(2,1)S(1)}, bf16[2,512,128]{2,1,0:T(8,128)(2,1)S(1)}, u32[]{:S(2)}, u32[]{:S(2)}) collective-permute-start(bf16[2,512,128]{2,1,0:T(8,128)(2,1)S(1)} %get-tuple-element.268), channel_id=1, source_target_pairs={{1,0},{2,1},{3,2},{4,3},{5,4},{6,5},{7,6},{8,7},{9,8},{10,9},{11,1... | collective-permute-start | bytes 786440 | tf_op jit(solution)/shard_map/ppermute | solution.py:19
  137.5 2.5 copy-start.4
  216.8 22.1 %collective-permute-start.5 = (bf16[2,128,512]{2,1,0:T(8,128)(2,1)S(1)}, bf16[2,128,512]{2,1,0:T(8,128)(2,1)S(1)}, u32[]{:S(2)}, u32[]{:S(2)}) collective-permute-start(bf16[2,128,512]{2,1,0:T(8,128)(2,1)S(1)} %get-tuple-element.263), channel_id=1, source_target_pairs={{0,16},{16,32},{32,48},{48,64},{64,80},{80,96},{96,112},{112,128},... | collective-permute-start | bytes 786440 | tf_op jit(solution)/shard_map/ppermute | solution.py:18
  218.7 21.6 %collective-permute-start.6 = (bf16[2,128,512]{2,1,0:T(8,128)(2,1)S(1)}, bf16[2,128,512]{2,1,0:T(8,128)(2,1)S(1)}, u32[]{:S(2)}, u32[]{:S(2)}) collective-permute-start(bf16[2,128,512]{2,1,0:T(8,128)(2,1)S(1)} %get-tuple-element.264), channel_id=1, source_target_pairs={{16,0},{32,16},{48,32},{64,48},{80,64},{96,80},{112,96},{128,112},... | collective-permute-start | bytes 786440 | tf_op jit(solution)/shard_map/ppermute | solution.py:19
  240.6 6.9 %collective-permute-start.7 = (bf16[2,256,128]{2,1,0:T(8,128)(2,1)S(1)}, bf16[2,256,128]{2,1,0:T(8,128)(2,1)S(1)}, u32[]{:S(2)}, u32[]{:S(2)}) collective-permute-start(bf16[2,256,128]{2,1,0:T(8,128)(2,1)S(1)} %get-tuple-element.265), channel_id=1, source_target_pairs={{0,1},{1,2},{2,3},{3,4},{4,5},{5,6},{6,7},{7,8},{8,9},{9,10},{10,1... | collective-permute-start | bytes 393224 | tf_op jit(solution)/shard_map/ppermute | solution.py:18
  241.9 7.9 %collective-permute-start.8 = (bf16[2,256,128]{2,1,0:T(8,128)(2,1)S(1)}, bf16[2,256,128]{2,1,0:T(8,128)(2,1)S(1)}, u32[]{:S(2)}, u32[]{:S(2)}) collective-permute-start(bf16[2,256,128]{2,1,0:T(8,128)(2,1)S(1)} %get-tuple-element.266), channel_id=1, source_target_pairs={{1,0},{2,1},{3,2},{4,3},{5,4},{6,5},{7,6},{8,7},{9,8},{10,9},{11,1... | collective-permute-start | bytes 393224 | tf_op jit(solution)/shard_map/ppermute | solution.py:19
  271.6 12.5 %collective-permute-start.9 = (bf16[12,2,16,256]{3,0,2,1:T(8,128)(2,1)S(1)}, bf16[12,2,16,256]{3,0,2,1:T(8,128)(2,1)S(1)}, u32[]{:S(2)}, u32[]{:S(2)}) collective-permute-start(bf16[12,2,16,256]{3,0,2,1:T(8,128)(2,1)S(1)} %copy.183), channel_id=1, source_target_pairs={{0,16},{16,32},{32,48},{48,64},{64,80},{80,96},{96,112},{112,128},... | collective-permute-start | bytes 589832 | tf_op jit(solution)/shard_map/ppermute | solution.py:27
  273.6 11.6 %copy-start = (f32[2,256,256]{2,1,0:T(8,128)}, f32[2,256,256]{2,1,0:T(8,128)S(1)}, u32[]{:S(2)}) copy-start(f32[2,256,256]{2,1,0:T(8,128)S(1)} %fusion.35) | copy-start | bytes 1572868
Sparse Core Ops, SparseCore 0:
  21.2 99.6 all-gather.1
  166.2 104.1 reduce-scatter.4
where the time goes:
time: 297 us; the launch traced here: 292 us
  waiting for transfers between devices  128 us (43%)
  local copies, waits for them, and re-layouts  51.7 us (17%)
  starting transfers between devices  38.6 us (13%)
  matrix products  37.5 us (13%)
  between operations  15.6 us (5%)
  other arithmetic  10.8 us (4%)
  loops' own time  10 us (3%)
    all_gather x1, waiting for transfers between devices, local(): portion = lax.all_gather(stacked, 'col', axis=2, tiled=True)  58.2 us
    dynamic_update_slice x4, local copies, waits for them, and re-layouts, place(): lax.dynamic_update_slice(accum, current + object_terms[position], (jnp.in...  31.2 us
    ppermute x4, waiting for transfers between devices, extended_2(): before = lax.ppermute(last, axis, up)  25 us
    unnamed x3, waiting for transfers between devices  20.6 us
    ppermute x4, starting transfers between devices, extended_2(): after = lax.ppermute(leading, axis, down)  18.9 us
    ppermute x2, waiting for transfers between devices, from_behind(): lax.ppermute(value, axis, [(source, source + steps) for source in range(l...  14.2 us
    dot_general x8, matrix products, multiply(): jnp.einsum('pmc,cn->pmn', operand, table, preferred_element_type=jnp.floa...  11.4 us
    ppermute x2, starting transfers between devices, from_behind(): lax.ppermute(value, axis, [(source, source + steps) for source in range(l...  10.3 us
  transfers between devices with their start and end apart: 12, of which 12 were waited for; matrix products, arithmetic and copies ran while one was open for 17% of the time, Pallas kernels for 0%

commit v1 on v0

v1 whole, which is shorter than its diff:
```python
import functools
import math

import jax
import jax.numpy as jnp
import numpy as np
from jax import lax
from jax.experimental import pallas as pl
from jax.experimental.pallas import tpu as pltpu
from jax.sharding import PartitionSpec as P

FLOOR = 0.25
PAD = 128
SLOT_ROWS = 8
F32 = jnp.float32
BF16 = jnp.bfloat16
MESH = pl.DeviceIdType.MESH


def dft_blocks(length):
    index = np.arange(length)
    angles = (index[:, None] * index[None, :] % length).astype(np.float32) * np.float32(2.0 * math.pi / length)
    scaling = np.float32(1.0 / math.sqrt(length))
    re = (np.cos(angles) * scaling).astype(jnp.bfloat16)
    im = (-np.sin(angles) * scaling).astype(jnp.bfloat16)
    block = np.block([[re, -im], [im, re]])
    return block, np.ascontiguousarray(block.T)


def dot(a, b):
    return jnp.dot(a, b, preferred_element_type=F32)


def iota(shape, dim):
    return lax.broadcasted_iota(jnp.int32, shape, dim)


def where_bf16(mask):
    return jnp.where(mask, 1.0, 0.0).astype(BF16)


def kernel(
    dims,
    place_ref, count_ref, object_ref, modes_ref, mix_ref, inten_hbm, m_hbm, mt_hbm,
    grad_ref, mode_ref,
    ext, nxt, mixes, stack, kron, kron_t, share, probes, windows, inten, m_ref, mt_ref,
    terms, got_terms, acc, out_cols, got_cols, out_rows, got_rows, sums, out_sums, got_sums,
    local_sem, pair_send, pair_recv, mix_send, mix_recv, probe_send, probe_recv, term_send, term_recv,
):
    rows, cols, slots, num_modes, strip = dims
    size = cols * strip
    half = size // 2
    full = 2 * size
    width = 2 * num_modes * strip
    r, c = lax.axis_index("row"), lax.axis_index("col")
    north, south = lax.rem(r + rows - 1, rows), lax.rem(r + 1, rows)
    west, east = lax.rem(c + cols - 1, cols), lax.rem(c + 1, cols)

    def remote(src, dst, index, device):
        return pltpu.make_async_remote_copy(
            src_ref=src, dst_ref=dst, send_sem=pair_send.at[index], recv_sem=pair_recv.at[index],
            device_id=device, device_id_type=MESH,
        )

    def everyone(body):
        def step(k, carry):
            body(lax.rem(c + k, cols))
            return carry

        lax.fori_loop(1, cols, step, 0)

    loads = [
        pltpu.make_async_copy(src, dst, local_sem.at[i])
        for i, (src, dst) in enumerate([(inten_hbm, inten), (m_hbm, m_ref), (mt_hbm, mt_ref)])
    ]
    for load in loads:
        load.start()

    barrier = pltpu.get_barrier_semaphore()
    everyone(lambda peer: pl.semaphore_signal(barrier, inc=1, device_id={"col": peer}, device_id_type=MESH))
    for peer in (north, south):
        pl.semaphore_signal(barrier, inc=1, device_id={"row": peer}, device_id_type=MESH)
    inner = pl.ds(half, size)
    low, high = pl.ds(half, half), pl.ds(size, half)
    first, last = pl.ds(0, half), pl.ds(size + half, half)
    ext[:, inner, inner] = object_ref[...].astype(BF16)
    mixes[c] = mix_ref[...]
    pl.semaphore_wait(barrier, cols + 1)

    send_modes = remote(modes_ref, nxt, 0, {"row": north})
    send_modes.start()

    def mix_copy(peer):
        return pltpu.make_async_remote_copy(
            src_ref=mix_ref, dst_ref=mixes.at[c], send_sem=mix_send, recv_sem=mix_recv,
            device_id={"col": peer}, device_id_type=MESH,
        )

    everyone(lambda peer: mix_copy(peer).start())
    to_north = remote(ext.at[:, low, inner], ext.at[:, last, inner], 1, {"row": north})
    to_south = remote(ext.at[:, high, inner], ext.at[:, first, inner], 2, {"row": south})
    to_west = remote(ext.at[:, inner, low], ext.at[:, inner, last], 3, {"col": west})
    to_east = remote(ext.at[:, inner, high], ext.at[:, inner, first], 4, {"col": east})
    for copy in (to_north, to_south, to_west, to_east):
        copy.start()

    others = pl.ds(0, cols - 1)
    pltpu.make_async_copy(mixes.at[others], mixes.at[others], mix_recv).wait()
    mixed = mixes[...].reshape(cols * SLOT_ROWS, PAD)
    coarse = mixed.astype(BF16)
    fine = (mixed - coarse.astype(F32)).astype(BF16)
    repeat = where_bf16(iota((PAD, width), 0) == lax.div(iota((PAD, width), 1), strip))
    diagonal = iota((strip, width), 0) == lax.rem(iota((strip, width), 1), strip)
    for i, part in enumerate((coarse, fine)):
        wide = dot(part, repeat).reshape(cols, SLOT_ROWS, width)
        for p in range(slots):
            block = jnp.where(diagonal[None], wide[:, p : p + 1, :], 0.0)
            kron[i, p] = block.reshape(size, width).astype(BF16)

    send_modes.wait_recv()
    for plane in range(2):
        lanes = pl.ds(plane * size, size)
        stack[: width // 2, lanes] = modes_ref[:, plane].reshape(width // 2, size)
        stack[width // 2 :, lanes] = nxt[:, plane].reshape(width // 2, size)

    def probe_copy(p, peer):
        return pltpu.make_async_remote_copy(
            src_ref=share.at[p, peer], dst_ref=probes.at[p, c], send_sem=probe_send.at[p], recv_sem=probe_recv.at[p],
            device_id={"col": peer}, device_id_type=MESH,
        )

    def mix_slot(p):
        both = dot(kron[0, p], stack[...]) + dot(kron[1, p], stack[...])
        for plane in range(2):
            part = both[:, plane * size : (plane + 1) * size].astype(BF16)
            share[p, :, plane] = part.reshape(cols, strip, size)
        probes[p, c] = share[p, c]
        everyone(lambda peer: probe_copy(p, peer).start())

    mix_slot(0)
    to_south.wait_recv()
    north_west = remote(ext.at[:, first, low], ext.at[:, first, last], 5, {"col": west})
    north_east = remote(ext.at[:, first, high], ext.at[:, first, first], 6, {"col": east})
    north_west.start()
    north_east.start()
    to_north.wait_recv()
    south_west = remote(ext.at[:, last, low], ext.at[:, last, last], 7, {"col": west})
    south_east = remote(ext.at[:, last, high], ext.at[:, last, first], 8, {"col": east})
    south_west.start()
    south_east.start()
    for p in range(1, slots):
        mix_slot(p)

    repeat_t = where_bf16(iota((width, PAD), 1) == lax.div(iota((width, PAD), 0), strip))
    diagonal_t = lax.rem(iota((width, size), 0), strip) == lax.rem(iota((width, size), 1), strip)
    for i, part in enumerate((coarse, fine)):
        wide_t = lax.dot_general(repeat_t, part, (((1,), (1,)), ((), ())), preferred_element_type=F32).astype(BF16)
        for p in range(slots):
            sel_shape = (cols * SLOT_ROWS, size)
            select = where_bf16(iota(sel_shape, 0) == lax.div(iota(sel_shape, 1), strip) * SLOT_ROWS + p)
            kron_t[i, p] = jnp.where(diagonal_t, dot(wide_t, select), 0.0).astype(BF16)
    acc[...] = jnp.zeros_like(acc)

    for copy in (to_west, to_east, north_west, north_east, south_west, south_east):
        copy.wait_recv()
    for copy in (to_north, to_south, to_west, to_east, north_west, north_east, south_west, south_east):
        copy.wait_send()
    for edge, box in (
        (r == 0, (slice(None), first, slice(None))),
        (r == rows - 1, (slice(None), last, slice(None))),
        (c == 0, (slice(None), pl.ds(0, full), first)),
        (c == cols - 1, (slice(None), pl.ds(0, full), last)),
    ):

        @pl.when(edge)
        def _(box=box):
            ext[box] = jnp.zeros_like(ext[box])

    def cut(p, carry):
        pick_rows = where_bf16(iota((size, full), 1) == iota((size, full), 0) + place_ref[p, 0])
        pick_cols = where_bf16(iota((full, size), 0) == iota((full, size), 1) + place_ref[p, 1])
        for plane in range(2):
            narrow = dot(ext[plane], pick_cols).astype(BF16)
            windows[p, plane] = dot(pick_rows, narrow).astype(BF16)
        return carry

    lax.fori_loop(0, slots, cut, 0)
    for load in loads:
        load.wait()

    def term_copy(p, peer):
        return pltpu.make_async_remote_copy(
            src_ref=terms.at[p, peer], dst_ref=got_terms.at[p, c], send_sem=term_send.at[p], recv_sem=term_recv.at[p],
            device_id={"col": peer}, device_id_type=MESH,
        )

    def position(p, carry):
        pltpu.make_async_copy(probes.at[p, others], probes.at[p, others], probe_recv.at[p]).wait()
        pr_re = probes[p, :, 0].reshape(size, size).astype(F32)
        pr_im = probes[p, :, 1].reshape(size, size).astype(F32)
        w_re = windows[p, 0].astype(F32)
        w_im = windows[p, 1].astype(F32)
        e_re = (pr_re * w_re - pr_im * w_im).astype(BF16)
        e_im = (pr_re * w_im + pr_im * w_re).astype(BF16)
        left = dot(m_ref[...], jnp.concatenate([e_re, e_im], axis=0)).astype(BF16)
        far = dot(jnp.concatenate([left[:size], left[size:]], axis=1), mt_ref[...])
        f_re, f_im = far[:, :size], far[:, size:]
        energy = jnp.maximum(f_re * f_re + f_im * f_im, FLOOR * FLOOR)
        live = jnp.where(p < count_ref[0, 0], 1.0, 0.0).astype(F32)
        factor = (jnp.sqrt(inten[p].astype(F32)) * lax.rsqrt(energy) - 1.0) * live
        c_re = (f_re * factor).astype(BF16)
        c_im = (f_im * factor).astype(BF16)
        back = dot(mt_ref[...], jnp.concatenate([c_re, c_im], axis=0)).astype(BF16)
        update = dot(jnp.concatenate([back[:size], back[size:]], axis=1), m_ref[...])
        u_re, u_im = update[:, :size], update[:, size:]
        terms[p, :, 0] = (w_re * u_re + w_im * u_im).astype(BF16).reshape(cols, strip, size)
        terms[p, :, 1] = (w_re * u_im - w_im * u_re).astype(BF16).reshape(cols, strip, size)
        got_terms[p, c] = terms[p, c]
        everyone(lambda peer: term_copy(p, peer).start())
        put_rows = where_bf16(iota((full, size), 0) == iota((full, size), 1) + place_ref[p, 0])
        put_cols = where_bf16(iota((size, full), 1) == iota((size, full), 0) + place_ref[p, 1])
        for plane, value in enumerate((pr_re * u_re + pr_im * u_im, pr_re * u_im - pr_im * u_re)):
            acc[plane] += dot(put_rows, dot(value.astype(BF16), put_cols).astype(BF16))
        return carry

    lax.fori_loop(0, slots, position, 0)

    out_cols[0] = acc[:, :, first].astype(BF16)
    out_cols[1] = acc[:, :, last].astype(BF16)
    cols_west = remote(out_cols.at[0], got_cols.at[1], 9, {"col": west})
    cols_east = remote(out_cols.at[1], got_cols.at[0], 10, {"col": east})
    cols_west.start()
    cols_east.start()

    def gather(p):
        pltpu.make_async_copy(got_terms.at[p, others], got_terms.at[p, others], term_recv.at[p]).wait()
        both = jnp.concatenate([got_terms[p, :, plane].reshape(size, size) for plane in range(2)], axis=1)
        return dot(kron_t[0, p], both) + dot(kron_t[1, p], both)

    sums[...] = gather(0)
    for p in range(1, slots - 1):
        sums[...] += gather(p)

    cols_east.wait_recv()
    acc[:, :, low] += jnp.where(c == 0, 0.0, got_cols[0].astype(F32))
    cols_west.wait_recv()
    acc[:, :, high] += jnp.where(c == cols - 1, 0.0, got_cols[1].astype(F32))
    out_rows[0] = acc[:, first, inner].astype(BF16)
    out_rows[1] = acc[:, last, inner].astype(BF16)
    rows_north = remote(out_rows.at[0], got_rows.at[1], 11, {"row": north})
    rows_south = remote(out_rows.at[1], got_rows.at[0], 12, {"row": south})
    rows_north.start()
    rows_south.start()

    sums[...] += gather(slots - 1)
    for plane in range(2):
        part = sums[width // 2 :, pl.ds(plane * size, size)].astype(BF16)
        out_sums[:, plane] = part.reshape(num_modes, strip, size)
    send_sums = remote(out_sums, got_sums, 13, {"row": south})
    send_sums.start()

    rows_south.wait_recv()
    grad_ref[:, pl.ds(0, half), :] = acc[:, low, inner] + jnp.where(r == 0, 0.0, got_rows[0].astype(F32))
    rows_north.wait_recv()
    grad_ref[:, pl.ds(half, half), :] = acc[:, high, inner] + jnp.where(r == rows - 1, 0.0, got_rows[1].astype(F32))
    send_sums.wait_recv()
    for plane in range(2):
        own = sums[: width // 2, pl.ds(plane * size, size)].reshape(num_modes, strip, size)
        mode_ref[:, plane] = own + got_sums[:, plane].astype(F32)

    for copy in (send_modes, cols_west, cols_east, rows_north, rows_south, send_sums):
        copy.wait_send()
    pltpu.make_async_copy(mixes.at[others], mixes.at[others], mix_send).wait()
    for p in range(slots):
        pltpu.make_async_copy(share.at[p, others], share.at[p, others], probe_send.at[p]).wait()
        pltpu.make_async_copy(terms.at[p, others], terms.at[p, others], term_send.at[p]).wait()


def local(object_field, modes, coeffs, offsets, region, counts, intensity):
    size = modes.shape[-1]
    half = size // 2
    full = 2 * size
    num_modes = modes.shape[1]
    slots = coeffs.shape[2]
    strip = modes.shape[3]
    rows, cols = lax.axis_size("row"), lax.axis_size("col")
    row_index = lax.axis_index("row")
    weights = coeffs[0, 0]
    regions = region[0, 0]
    own_mask = (regions == row_index).astype(F32)
    next_mask = (regions == row_index + 1).astype(F32)
    mixing = jnp.concatenate([weights * own_mask[:, None], weights * next_mask[:, None]], axis=1)
    mixing = jnp.pad(mixing, ((0, SLOT_ROWS - slots), (0, PAD - 2 * num_modes)))
    place = offsets[0, 0] + half
    block, block_t = dft_blocks(size)
    width = 2 * num_modes * strip
    vmem = pl.BlockSpec(memory_space=pltpu.VMEM)
    smem = pl.BlockSpec(memory_space=pltpu.SMEM)
    hbm = pl.BlockSpec(memory_space=pl.ANY)
    pieces = (slots, cols, 2, strip, size)
    dma = pltpu.SemaphoreType.DMA
    object_grad, mode_grad = pl.pallas_call(
        functools.partial(kernel, (rows, cols, slots, num_modes, strip)),
        out_shape=(
            jax.ShapeDtypeStruct((2, size, size), F32),
            jax.ShapeDtypeStruct((num_modes, 2, strip, size), F32),
        ),
        in_specs=[smem, smem, vmem, vmem, vmem, hbm, hbm, hbm],
        out_specs=(vmem, vmem),
        scratch_shapes=[
            pltpu.VMEM((2, full, full), BF16),
            pltpu.VMEM((num_modes, 2, strip, size), BF16),
            pltpu.VMEM((cols, SLOT_ROWS, PAD), F32),
            pltpu.VMEM((width, full), BF16),
            pltpu.VMEM((2, slots, size, width), BF16),
            pltpu.VMEM((2, slots, width, size), BF16),
            pltpu.VMEM(pieces, BF16),
            pltpu.VMEM(pieces, BF16),
            pltpu.VMEM((slots, 2, size, size), BF16),
            pltpu.VMEM((slots, size, size), BF16),
            pltpu.VMEM((full, full), BF16),
            pltpu.VMEM((full, full), BF16),
            pltpu.VMEM(pieces, BF16),
            pltpu.VMEM(pieces, BF16),
            pltpu.VMEM((2, full, full), F32),
            pltpu.VMEM((2, 2, full, half), BF16),
            pltpu.VMEM((2, 2, full, half), BF16),
            pltpu.VMEM((2, 2, half, size), BF16),
            pltpu.VMEM((2, 2, half, size), BF16),
            pltpu.VMEM((width, full), F32),
            pltpu.VMEM((num_modes, 2, strip, size), BF16),
            pltpu.VMEM((num_modes, 2, strip, size), BF16),
            dma((3,)),
            dma((14,)),
            dma((14,)),
            dma,
            dma,
            dma((slots,)),
            dma((slots,)),
            dma((slots,)),
            dma((slots,)),
        ],
        compiler_params=pltpu.CompilerParams(
            collective_id=0, has_side_effects=True, vmem_limit_bytes=56 << 20
        ),
        name="ptychography",
    )(place, counts, object_field, modes[0], mixing, intensity[0, 0], jnp.asarray(block), jnp.asarray(block_t))
    return object_grad, mode_grad[None]


def solution(mesh):
    in_specs = (
        P(None, "row", "col"),
        P("row", None, None, "col", None),
        P("row", "col", None, None),
        P("row", "col", None, None),
        P("row", "col", None),
        P("row", "col"),
        P("row", "col", None, None, None),
    )
    out_specs = (P(None, "row", "col"), P("row", None, None, "col", None))
    return jax.shard_map(local, mesh=mesh, in_specs=in_specs, out_specs=out_specs, check_vma=False)
```

time: 297 us -> 103 us (0.35)
  the two profiles are of different devices: /device:TPU:16 before, /device:TPU:208 now
where the time goes in v1:
time: 103 us
  Pallas kernels  96.5 us (94%)
  local copies, waits for them, and re-layouts  4.68 us (5%)
  between operations  1.31 us (1%)
    pallas_call x1, Pallas kernels, local(): pl.pallas_call(functools.partial(kernel, (rows, cols, slots, num_modes, s...  96.5 us
    unnamed x10, local copies, waits for them, and re-layouts  4.01 us

profile of v1, /device:TPU:208, one launch (start us, length us, event | category | flops | bytes accessed | tf_op | source)
XLA Modules:
  0.0 103.3 jit_solution(16336325763439595894)
XLA Ops:
  1.3 0.0 copy-start.3
  1.3 0.6 copy-done.3
  1.9 0.0 copy-start.2
  1.9 0.7 copy-done.2
  2.6 0.0 copy-start.1
  2.6 0.7 copy.11.place_ref
  3.3 0.0 copy-done.1
  3.3 0.1 bitcast_multiply_fusion.1
  3.4 0.7 select_maximum_fusion.mix_ref
  4.0 96.5 %ptychography.1 = (f32[2,256,256]{2,1,0:T(8,128)}, f32[12,2,16,256]{3,2,1,0:T(8,128)}) custom-call(s32[4,2]{1,0:T(4,128)} %copy.11.place_ref, s32[1,1]{1,0:T(1,128)S(6)} %copy.14.count_ref, f32[2,256,256]{2,1,0:T(8,128)} %object_ref.1, bf16[12,2,16,256]{3,2,1,0:T(8,128)(2,1)} %bitcast.14, f32[8,128]{1,0:T(8,128)} %select_maximum_fusion.mix_ref, ...), custom_call_target="tpu_custom_call" | custom-call | tf_op jit(solution)/shard_map/ptychography/pallas_call | solution.py:302
  100.6 0.0 copy-start
  100.6 1.9 %copy.15 = f32[2,256,256]{2,1,0:T(8,128)} copy(f32[2,256,256]{2,1,0:T(8,128)} %get-tuple-element.12) | data formatting | bytes 1048576
  102.5 0.0 copy-done
  102.5 0.7 copy.16
  (2 shorter events, 0.0 us)
Async XLA Ops:
  1.3 0.7 copy-start.3
  1.9 0.7 copy-start.2
  2.6 0.7 copy-start.1
  100.6 1.9 %copy-start = (f32[12,2,16,256]{3,2,1,0:T(8,128)S(1)}, f32[12,2,16,256]{3,2,1,0:T(8,128)}, u32[]{:S(2)}) copy-start(f32[12,2,16,256]{3,2,1,0:T(8,128)} %get-tuple-element.5) | copy-start | bytes 1179652

commit v2 on v1

v2 whole, which is shorter than its diff:
```python
import functools
import math

import jax
import jax.numpy as jnp
import numpy as np
from jax import lax
from jax.experimental import pallas as pl
from jax.experimental.pallas import tpu as pltpu
from jax.sharding import PartitionSpec as P

FLOOR = 0.25
PAD = 128
SLOT_ROWS = 8
F32 = jnp.float32
BF16 = jnp.bfloat16
MESH = pl.DeviceIdType.MESH


def dft_blocks(length):
    index = np.arange(length)
    angles = (index[:, None] * index[None, :] % length).astype(np.float32) * np.float32(2.0 * math.pi / length)
    scaling = np.float32(1.0 / math.sqrt(length))
    re = (np.cos(angles) * scaling).astype(jnp.bfloat16)
    im = (-np.sin(angles) * scaling).astype(jnp.bfloat16)
    block = np.block([[re, -im], [im, re]])
    return block, np.ascontiguousarray(block.T)


def dot(a, b):
    return jnp.dot(a, b, preferred_element_type=F32)


def iota(shape, dim):
    return lax.broadcasted_iota(jnp.int32, shape, dim)


def where_bf16(mask):
    return jnp.where(mask, 1.0, 0.0).astype(BF16)


def kernel(
    dims,
    object_hbm, modes_hbm, coeffs_hbm, offsets_hbm, region_hbm, counts_hbm, inten_hbm, m_hbm, mt_hbm,
    grad_ref, mode_ref,
    object_ref, modes_ref, coeffs_ref, offsets_ref, region_ref, counts_ref, inten, m_ref, mt_ref,
    ext, nxt, mixes, stack, kron, kron_t, share, probes, windows,
    terms, got_terms, acc, out_cols, got_cols, out_rows, got_rows, sums, out_sums, got_sums,
    local_sem, pair_send, pair_recv, mix_send, mix_recv, probe_send, probe_recv, term_send, term_recv,
):
    rows, cols, slots, num_modes, strip = dims
    size = cols * strip
    half = size // 2
    full = 2 * size
    split = num_modes * strip
    width = 2 * split
    r, c = lax.axis_index("row"), lax.axis_index("col")
    north, south = lax.rem(r + rows - 1, rows), lax.rem(r + 1, rows)
    west, east = lax.rem(c + cols - 1, cols), lax.rem(c + 1, cols)
    inner = pl.ds(half, size)
    low, high = pl.ds(half, half), pl.ds(size, half)
    first, last = pl.ds(0, half), pl.ds(size + half, half)
    others = pl.ds(0, cols - 1)

    def remote(src, dst, index, device):
        return pltpu.make_async_remote_copy(
            src_ref=src, dst_ref=dst, send_sem=pair_send.at[index], recv_sem=pair_recv.at[index],
            device_id=device, device_id_type=MESH,
        )

    def scatter(src, dst, send_sem, recv_sem, peer):
        return pltpu.make_async_remote_copy(
            src_ref=src, dst_ref=dst, send_sem=send_sem, recv_sem=recv_sem,
            device_id={"col": peer}, device_id_type=MESH,
        )

    def everyone(body):
        def step(k, carry):
            body(lax.rem(c + k, cols))
            return carry

        lax.fori_loop(1, cols, step, 0)

    def arrived(buffer, sem):
        pltpu.make_async_copy(buffer, buffer, sem).wait()

    barrier = pltpu.get_barrier_semaphore()
    everyone(lambda peer: pl.semaphore_signal(barrier, inc=1, device_id={"col": peer}, device_id_type=MESH))
    for peer in (north, south):
        pl.semaphore_signal(barrier, inc=1, device_id={"row": peer}, device_id_type=MESH)
    pairs = [
        (coeffs_hbm, coeffs_ref), (region_hbm, region_ref), (modes_hbm, modes_ref), (object_hbm, object_ref),
        (offsets_hbm, offsets_ref), (counts_hbm, counts_ref), (inten_hbm, inten), (m_hbm, m_ref), (mt_hbm, mt_ref),
    ]
    loads = [pltpu.make_async_copy(src, dst, local_sem.at[i]) for i, (src, dst) in enumerate(pairs)]
    for load in loads:
        load.start()
    for load in loads[:2]:
        load.wait()
    mixes[c] = jnp.zeros((SLOT_ROWS, PAD), F32)
    for p in range(slots):
        weights = coeffs_ref[0, 0, p : p + 1, :]
        area = region_ref[0, :, p : p + 1]
        mixes[c, p : p + 1, :num_modes] = jnp.where(area == r, weights, 0.0)
        mixes[c, p : p + 1, num_modes : 2 * num_modes] = jnp.where(area == r + 1, weights, 0.0)
    for load in loads[2:4]:
        load.wait()
    ext[:, inner, inner] = object_ref[...].astype(BF16)
    pl.semaphore_wait(barrier, cols + 1)

    everyone(lambda peer: scatter(mixes.at[c], mixes.at[c], mix_send, mix_recv, peer).start())
    send_modes = remote(modes_ref, nxt, 0, {"row": north})
    send_modes.start()
    to_north = remote(ext.at[:, low, inner], ext.at[:, last, inner], 1, {"row": north})
    to_south = remote(ext.at[:, high, inner], ext.at[:, first, inner], 2, {"row": south})
    to_west = remote(ext.at[:, inner, low], ext.at[:, inner, last], 3, {"col": west})
    to_east = remote(ext.at[:, inner, high], ext.at[:, inner, first], 4, {"col": east})
    for copy in (to_north, to_south, to_west, to_east):
        copy.start()

    def stack_modes(modes, start):
        for plane in range(2):
            stack[start : start + split, pl.ds(plane * size, size)] = modes[:, plane].reshape(split, size)

    stack_modes(modes_ref.at[0], 0)
    stack[split:] = jnp.zeros((split, full), BF16)

    arrived(mixes.at[others], mix_recv)
    mixed = mixes[...].reshape(cols * SLOT_ROWS, PAD)
    coarse = mixed.astype(BF16)
    fine = (mixed - coarse.astype(F32)).astype(BF16)
    repeat = where_bf16(iota((PAD, width), 0) == lax.div(iota((PAD, width), 1), strip))
    diagonal = iota((strip, width), 0) == lax.rem(iota((strip, width), 1), strip)
    for i, part in enumerate((coarse, fine)):
        wide = dot(part, repeat).reshape(cols, SLOT_ROWS, width)
        for p in range(slots):
            block = jnp.where(diagonal[None], wide[:, p : p + 1, :], 0.0)
            kron[i, p] = block.reshape(size, width).astype(BF16)

    def mix_slot(p):
        both = dot(kron[0, p], stack[...]) + dot(kron[1, p], stack[...])
        for plane in range(2):
            part = both[:, plane * size : (plane + 1) * size].astype(BF16)
            share[p, :, plane] = part.reshape(cols, strip, size)
        everyone(
            lambda peer: scatter(share.at[p, peer], probes.at[p, c], probe_send.at[p], probe_recv.at[p], peer).start()
        )
        probes[p, c] = share[p, c]

    mix_slot(0)
    send_modes.wait_recv()
    stack_modes(nxt.at[0], split)
    mix_slot(1)
    to_south.wait_recv()
    north_west = remote(ext.at[:, first, low], ext.at[:, first, last], 5, {"col": west})
    north_east = remote(ext.at[:, first, high], ext.at[:, first, first], 6, {"col": east})
    north_west.start()
    north_east.start()
    to_north.wait_recv()
    south_west = remote(ext.at[:, last, low], ext.at[:, last, last], 7, {"col": west})
    south_east = remote(ext.at[:, last, high], ext.at[:, last, first], 8, {"col": east})
    south_west.start()
    south_east.start()
    for p in range(2, slots):
        mix_slot(p)

    repeat_t = where_bf16(iota((width, PAD), 1) == lax.div(iota((width, PAD), 0), strip))
    diagonal_t = lax.rem(iota((width, size), 0), strip) == lax.rem(iota((width, size), 1), strip)
    for i, part in enumerate((coarse, fine)):
        wide_t = lax.dot_general(repeat_t, part, (((1,), (1,)), ((), ())), preferred_element_type=F32).astype(BF16)
        for p in range(slots):
            sel_shape = (cols * SLOT_ROWS, size)
            select = where_bf16(iota(sel_shape, 0) == lax.div(iota(sel_shape, 1), strip) * SLOT_ROWS + p)
            kron_t[i, p] = jnp.where(diagonal_t, dot(wide_t, select), 0.0).astype(BF16)
    acc[...] = jnp.zeros_like(acc)
    for load in loads[4:]:
        load.wait()

    for copy in (to_west, to_east, north_west, north_east, south_west, south_east):
        copy.wait_recv()
    for copy in (to_north, to_south, to_west, to_east, north_west, north_east, south_west, south_east):
        copy.wait_send()
    for edge, box in (
        (r == 0, (slice(None), first, slice(None))),
        (r == rows - 1, (slice(None), last, slice(None))),
        (c == 0, (slice(None), pl.ds(0, full), first)),
        (c == cols - 1, (slice(None), pl.ds(0, full), last)),
    ):

        @pl.when(edge)
        def _(box=box):
            ext[box] = jnp.zeros_like(ext[box])

    def corner(p, axis):
        return offsets_ref[0, 0, axis : axis + 1, p : p + 1] + half

    for p in range(slots):
        pick_rows = where_bf16(iota((size, full), 1) == iota((size, full), 0) + corner(p, 0))
        pick_cols = where_bf16(iota((full, size), 0) == iota((full, size), 1) + corner(p, 1))
        for plane in range(2):
            narrow = dot(ext[plane], pick_cols).astype(BF16)
            windows[p, plane] = dot(pick_rows, narrow).astype(BF16)

    def send_terms(p):
        everyone(
            lambda peer: scatter(terms.at[p, peer], got_terms.at[p, c], term_send.at[p], term_recv.at[p], peer).start()
        )
        got_terms[p, c] = terms[p, c]

    def position(p):
        arrived(probes.at[p, others], probe_recv.at[p])
        pr_re = probes[p, :, 0].reshape(size, size).astype(F32)
        pr_im = probes[p, :, 1].reshape(size, size).astype(F32)
        w_re = windows[p, 0].astype(F32)
        w_im = windows[p, 1].astype(F32)
        e_re = (pr_re * w_re - pr_im * w_im).astype(BF16)
        e_im = (pr_re * w_im + pr_im * w_re).astype(BF16)
        left = dot(m_ref[...], jnp.concatenate([e_re, e_im], axis=0)).astype(BF16)
        far = dot(jnp.concatenate([left[:size], left[size:]], axis=1), mt_ref[...])
        f_re, f_im = far[:, :size], far[:, size:]
        energy = jnp.maximum(f_re * f_re + f_im * f_im, FLOOR * FLOOR)
        live = jnp.where(counts_ref[...] > p, 1.0, 0.0)
        factor = (jnp.sqrt(inten[0, 0, p].astype(F32)) * lax.rsqrt(energy) - 1.0) * live
        c_re = (f_re * factor).astype(BF16)
        c_im = (f_im * factor).astype(BF16)
        back = dot(mt_ref[...], jnp.concatenate([c_re, c_im], axis=0)).astype(BF16)
        update = dot(jnp.concatenate([back[:size], back[size:]], axis=1), m_ref[...])
        u_re, u_im = update[:, :size], update[:, size:]
        terms[p, :, 0] = (w_re * u_re + w_im * u_im).astype(BF16).reshape(cols, strip, size)
        terms[p, :, 1] = (w_re * u_im - w_im * u_re).astype(BF16).reshape(cols, strip, size)
        if p < slots - 1:
            send_terms(p)
        put_rows = where_bf16(iota((full, size), 0) == iota((full, size), 1) + corner(p, 0))
        put_cols = where_bf16(iota((size, full), 1) == iota((size, full), 0) + corner(p, 1))
        for plane, value in enumerate((pr_re * u_re + pr_im * u_im, pr_re * u_im - pr_im * u_re)):
            acc[plane] += dot(put_rows, dot(value.astype(BF16), put_cols).astype(BF16))

    for p in range(slots):
        position(p)

    out_cols[0] = acc[:, :, first].astype(BF16)
    out_cols[1] = acc[:, :, last].astype(BF16)
    cols_west = remote(out_cols.at[0], got_cols.at[1], 9, {"col": west})
    cols_east = remote(out_cols.at[1], got_cols.at[0], 10, {"col": east})
    cols_west.start()
    cols_east.start()
    send_terms(slots - 1)

    def gather(p, half_of):
        both = jnp.concatenate([got_terms[p, :, plane].reshape(size, size) for plane in range(2)], axis=1)
        spot = pl.ds(half_of * split, split)
        value = dot(kron_t[0, p, spot], both) + dot(kron_t[1, p, spot], both)
        if p == 0:
            sums[spot] = value
        else:
            sums[spot] += value

    for p in range(slots - 2):
        arrived(got_terms.at[p, others], term_recv.at[p])
        gather(p, 1)

    cols_east.wait_recv()
    acc[:, :, low] += jnp.where(c == 0, 0.0, got_cols[0].astype(F32))
    cols_west.wait_recv()
    acc[:, :, high] += jnp.where(c == cols - 1, 0.0, got_cols[1].astype(F32))
    out_rows[0] = acc[:, first, inner].astype(BF16)
    out_rows[1] = acc[:, last, inner].astype(BF16)
    rows_north = remote(out_rows.at[0], got_rows.at[1], 11, {"row": north})
    rows_south = remote(out_rows.at[1], got_rows.at[0], 12, {"row": south})
    rows_north.start()
    rows_south.start()

    for p in range(slots - 2, slots):
        arrived(got_terms.at[p, others], term_recv.at[p])
        gather(p, 1)
    for plane in range(2):
        part = sums[split:, pl.ds(plane * size, size)].astype(BF16)
        out_sums[:, plane] = part.reshape(num_modes, strip, size)
    send_sums = remote(out_sums, got_sums, 13, {"row": south})
    send_sums.start()
    for p in range(slots):
        gather(p, 0)

    rows_south.wait_recv()
    grad_ref[:, pl.ds(0, half), :] = acc[:, low, inner] + jnp.where(r == 0, 0.0, got_rows[0].astype(F32))
    rows_north.wait_recv()
    grad_ref[:, pl.ds(half, half), :] = acc[:, high, inner] + jnp.where(r == rows - 1, 0.0, got_rows[1].astype(F32))
    send_sums.wait_recv()
    for plane in range(2):
        own = sums[:split, pl.ds(plane * size, size)].reshape(num_modes, strip, size)
        mode_ref[0, :, plane] = own + got_sums[:, plane].astype(F32)

    for copy in (send_modes, cols_west, cols_east, rows_north, rows_south, send_sums):
        copy.wait_send()
    arrived(mixes.at[others], mix_send)
    for p in range(slots):
        arrived(share.at[p, others], probe_send.at[p])
        arrived(terms.at[p, others], term_send.at[p])


def local(object_field, modes, coeffs, offsets, region, counts, intensity):
    size = modes.shape[-1]
    half = size // 2
    full = 2 * size
    num_modes = modes.shape[1]
    slots = coeffs.shape[2]
    strip = modes.shape[3]
    rows, cols = lax.axis_size("row"), lax.axis_size("col")
    block, block_t = dft_blocks(size)
    width = 2 * num_modes * strip
    vmem = pl.BlockSpec(memory_space=pltpu.VMEM)
    hbm = pl.BlockSpec(memory_space=pl.ANY)
    pieces = (slots, cols, 2, strip, size)
    dma = pltpu.SemaphoreType.DMA
    args = (
        object_field, modes, coeffs, jnp.swapaxes(offsets, 2, 3), region, counts, intensity, jnp.asarray(block), jnp.asarray(block_t),
    )
    return pl.pallas_call(
        functools.partial(kernel, (rows, cols, slots, num_modes, strip)),
        out_shape=(
            jax.ShapeDtypeStruct((2, size, size), F32),
            jax.ShapeDtypeStruct((1, num_modes, 2, strip, size), F32),
        ),
        in_specs=[hbm] * len(args),
        out_specs=(vmem, vmem),
        scratch_shapes=[pltpu.VMEM(x.shape, x.dtype) for x in args]
        + [
            pltpu.VMEM((2, full, full), BF16),
            pltpu.VMEM(modes.shape, BF16),
            pltpu.VMEM((cols, SLOT_ROWS, PAD), F32),
            pltpu.VMEM((width, full), BF16),
            pltpu.VMEM((2, slots, size, width), BF16),
            pltpu.VMEM((2, slots, width, size), BF16),
            pltpu.VMEM(pieces, BF16),
            pltpu.VMEM(pieces, BF16),
            pltpu.VMEM((slots, 2, size, size), BF16),
            pltpu.VMEM(pieces, BF16),
            pltpu.VMEM(pieces, BF16),
            pltpu.VMEM((2, full, full), F32),
            pltpu.VMEM((2, 2, full, half), BF16),
            pltpu.VMEM((2, 2, full, half), BF16),
            pltpu.VMEM((2, 2, half, size), BF16),
            pltpu.VMEM((2, 2, half, size), BF16),
            pltpu.VMEM((width, full), F32),
            pltpu.VMEM((num_modes, 2, strip, size), BF16),
            pltpu.VMEM((num_modes, 2, strip, size), BF16),
            dma((len(args),)),
            dma((14,)),
            dma((14,)),
            dma,
            dma,
            dma((slots,)),
            dma((slots,)),
            dma((slots,)),
            dma((slots,)),
        ],
        compiler_params=pltpu.CompilerParams(
            collective_id=0, has_side_effects=True, vmem_limit_bytes=56 << 20
        ),
        name="ptychography",
    )(*args)


def solution(mesh):
    in_specs = (
        P(None, "row", "col"),
        P("row", None, None, "col", None),
        P("row", "col", None, None),
        P("row", "col", None, None),
        P("row", "col", None),
        P("row", "col"),
        P("row", "col", None, None, None),
    )
    out_specs = (P(None, "row", "col"), P("row", None, None, "col", None))
    return jax.shard_map(local, mesh=mesh, in_specs=in_specs, out_specs=out_specs, check_vma=False)
```

time: 103 us -> 98.5 us (0.956)
  the two profiles are of different devices: /device:TPU:208 before, /device:TPU:64 now
where the time goes in v2:
time: 98.5 us; the launch traced here: 98.4 us
  Pallas kernels  94.4 us (96%)
  local copies, waits for them, and re-layouts  2.67 us (3%)
  between operations  1.3 us (1%)
    pallas_call x1, Pallas kernels, local(): pl.pallas_call(functools.partial(kernel, (rows, cols, slots, num_modes, s...  94.4 us
    unnamed x4, local copies, waits for them, and re-layouts  2.67 us

profile of v2, /device:TPU:64, one launch (start us, length us, event | category | flops | bytes accessed | tf_op | source)
XLA Modules:
  0.0 98.4 jit_solution(16087982042921825222)
XLA Ops:
  1.3 94.4 %ptychography.1 = (f32[2,256,256]{2,1,0:T(8,128)}, f32[1,12,2,16,256]{4,3,2,1,0:T(8,128)}) custom-call(f32[2,256,256]{2,1,0:T(8,128)} %object_hbm.1, bf16[1,12,2,16,256]{4,3,2,1,0:T(8,128)(2,1)} %modes_hbm.1, f32[1,1,4,12]{3,2,1,0:T(4,128)} %coeffs_hbm.1, s32[1,1,2,4]{3,2,1,0:T(2,128)} %bitcast.1, s32[1,1,4]{2,1,0:T(1,128)} %region_hbm.1, ...), custom_call_target="tpu_custom_call" | custom-call | tf_op jit(solution)/shard_map/ptychography/pallas_call | solution.py:318
  95.7 0.0 copy-start
  95.7 1.9 %copy.14 = f32[2,256,256]{2,1,0:T(8,128)} copy(f32[2,256,256]{2,1,0:T(8,128)} %get-tuple-element.4) | data formatting | bytes 1048576
  97.6 0.0 copy-done
  97.6 0.7 copy.15
Async XLA Ops:
  95.7 1.9 %copy-start = (f32[1,12,2,16,256]{4,3,2,1,0:T(8,128)S(1)}, f32[1,12,2,16,256]{4,3,2,1,0:T(8,128)}, u32[]{:S(2)}) copy-start(f32[1,12,2,16,256]{4,3,2,1,0:T(8,128)} %get-tuple-element.5) | copy-start | bytes 1179652

commit v3 on v2

--- a/solution.py
+++ b/solution.py
@@ -45,6 +45,7 @@
     grad_ref, mode_ref,
     object_ref, modes_ref, coeffs_ref, offsets_ref, region_ref, counts_ref, inten, m_ref, mt_ref,
     ext, nxt, mixes, stack, kron, kron_t, share, probes, windows,
+    help_own, help_nxt, help_stack, help_share, carried, carried_out,
     terms, got_terms, acc, out_cols, got_cols, out_rows, got_rows, sums, out_sums, got_sums,
     local_sem, pair_send, pair_recv, mix_send, mix_recv, probe_send, probe_recv, term_send, term_recv,
 ):
@@ -61,12 +62,32 @@
     low, high = pl.ds(half, half), pl.ds(size, half)
     first, last = pl.ds(0, half), pl.ds(size + half, half)
     others = pl.ds(0, cols - 1)
-
-    def remote(src, dst, index, device):
+    side = cols // 4
+    block = cols // 2
+    plane, spot = lax.div(c, side), lax.rem(c, side)
+    group = lax.div(c, block)
+    outer = (plane == 0) | (plane == 3)
+    helper = (plane == 1) | (plane == 2)
+    across = lax.rem(c + block, cols)
+    even = lax.rem(r, 2) == 0
+    has_west, has_east = c > 0, c < cols - 1
+    turn_west = (spot == 0) & has_west
+    turn_east = (spot == side - 1) & has_east
+    carry_west = (spot == side - 1) & (plane > 0)
+    carry_east = (spot == 0) & (plane < 3)
+
+    def remote(src, dst, index, device, sender=None):
         return pltpu.make_async_remote_copy(
-            src_ref=src, dst_ref=dst, send_sem=pair_send.at[index], recv_sem=pair_recv.at[index],
+            src_ref=src, dst_ref=dst,
+            send_sem=pair_send.at[index if sender is None else sender], recv_sem=pair_recv.at[index],
             device_id=device, device_id_type=MESH,
         )
+
+    def when(condition, *actions):
+        @pl.when(condition)
+        def _():
+            for action in actions:
+                action()
 
     def scatter(src, dst, send_sem, recv_sem, peer):
         return pltpu.make_async_remote_copy(
@@ -81,6 +102,13 @@
 
         lax.fori_loop(1, cols, step, 0)
 
+    def half_of(index, start, body):
+        def step(k, carry):
+            body(index * block + lax.rem(c + k, block))
+            return carry
+
+        lax.fori_loop(start, block, step, 0)
+
     def arrived(buffer, sem):
         pltpu.make_async_copy(buffer, buffer, sem).wait()
 
@@ -88,6 +116,8 @@
     everyone(lambda peer: pl.semaphore_signal(barrier, inc=1, device_id={"col": peer}, device_id_type=MESH))
     for peer in (north, south):
         pl.semaphore_signal(barrier, inc=1, device_id={"row": peer}, device_id_type=MESH)
+
+    pl.semaphore_signal(barrier, inc=1, device_id={"row": south, "col": across}, device_id_type=MESH)
     pairs = [
         (coeffs_hbm, coeffs_ref), (region_hbm, region_ref), (modes_hbm, modes_ref), (object_hbm, object_ref),
         (offsets_hbm, offsets_ref), (counts_hbm, counts_ref), (inten_hbm, inten), (m_hbm, m_ref), (mt_hbm, mt_ref),
@@ -106,24 +136,39 @@
     for load in loads[2:4]:
         load.wait()
     ext[:, inner, inner] = object_ref[...].astype(BF16)
-    pl.semaphore_wait(barrier, cols + 1)
+    pl.semaphore_wait(barrier, cols + 2)
 
     everyone(lambda peer: scatter(mixes.at[c], mixes.at[c], mix_send, mix_recv, peer).start())
     send_modes = remote(modes_ref, nxt, 0, {"row": north})
+    help_modes = remote(modes_ref, help_own, 14, {"row": r, "col": across})
+    help_next = remote(modes_ref, help_nxt, 15, {"row": north, "col": across})
+    help_pass = remote(help_own, help_nxt, 15, {"row": north})
+    when(outer, help_modes.start)
     send_modes.start()
+    when(outer & even, help_next.start)
     to_north = remote(ext.at[:, low, inner], ext.at[:, last, inner], 1, {"row": north})
     to_south = remote(ext.at[:, high, inner], ext.at[:, first, inner], 2, {"row": south})
     to_west = remote(ext.at[:, inner, low], ext.at[:, inner, last], 3, {"col": west})
     to_east = remote(ext.at[:, inner, high], ext.at[:, inner, first], 4, {"col": east})
-    for copy in (to_north, to_south, to_west, to_east):
-        copy.start()
-
-    def stack_modes(modes, start):
-        for plane in range(2):
-            stack[start : start + split, pl.ds(plane * size, size)] = modes[:, plane].reshape(split, size)
-
-    stack_modes(modes_ref.at[0], 0)
+    west_turn = remote(ext.at[:, inner, low], carried.at[0], 16, {"col": c + side - 1})
+    east_turn = remote(ext.at[:, inner, high], carried.at[1], 17, {"col": c - side + 1})
+    west_pass = remote(carried.at[0], ext.at[:, inner, last], 3, {"col": c - side}, 18)
+    east_pass = remote(carried.at[1], ext.at[:, inner, first], 4, {"col": c + side}, 19)
+    go_west, go_east = has_west & (spot > 0), has_east & (spot < side - 1)
+    when(turn_west, west_turn.start)
+    when(turn_east, east_turn.start)
+    to_north.start()
+    to_south.start()
+    when(go_west, to_west.start)
+    when(go_east, to_east.start)
+
+    def stack_modes(stack, modes, start):
+        for part in range(2):
+            stack[start : start + split, pl.ds(part * size, size)] = modes[0, :, part].reshape(split, size)
+
+    stack_modes(stack, modes_ref, 0)
     stack[split:] = jnp.zeros((split, full), BF16)
+    help_stack[split:] = jnp.zeros((split, full), BF16)
 
     arrived(mixes.at[others], mix_recv)
     mixed = mixes[...].reshape(cols * SLOT_ROWS, PAD)
@@ -134,35 +179,66 @@
     for i, part in enumerate((coarse, fine)):
         wide = dot(part, repeat).reshape(cols, SLOT_ROWS, width)
         for p in range(slots):
-            block = jnp.where(diagonal[None], wide[:, p : p + 1, :], 0.0)
-            kron[i, p] = block.reshape(size, width).astype(BF16)
+            spread = jnp.where(diagonal[None], wide[:, p : p + 1, :], 0.0)
+            kron[i, p] = spread.reshape(size, width).astype(BF16)
+
+    def probe_copy(share, p, index, strip_index, peer):
+        return scatter(share.at[p, index], probes.at[p, strip_index], probe_send.at[p], probe_recv.at[p], peer)
 
     def mix_slot(p):
         both = dot(kron[0, p], stack[...]) + dot(kron[1, p], stack[...])
-        for plane in range(2):
-            part = both[:, plane * size : (plane + 1) * size].astype(BF16)
-            share[p, :, plane] = part.reshape(cols, strip, size)
-        everyone(
-            lambda peer: scatter(share.at[p, peer], probes.at[p, c], probe_send.at[p], probe_recv.at[p], peer).start()
-        )
+        for part in range(2):
+            value = both[:, part * size : (part + 1) * size].astype(BF16)
+            share[p, :, part] = value.reshape(cols, strip, size)
+        half_of(group, 1, lambda peer: probe_copy(share, p, peer, c, peer).start())
+        when(helper, lambda: half_of(1 - group, 0, lambda peer: probe_copy(share, p, peer, c, peer).start()))
         probes[p, c] = share[p, c]
 
+    def help_slot(p):
+        @pl.when(helper)
+        def _():
+            lines = pl.ds(pl.multiple_of(group * half, half), half)
+            both = dot(kron[0, p, lines], help_stack[...]) + dot(kron[1, p, lines], help_stack[...])
+            for part in range(2):
+                value = both[:, part * size : (part + 1) * size].astype(BF16)
+                help_share[p, :, part] = value.reshape(block, strip, size)
+            half_of(group, 1, lambda peer: probe_copy(help_share, p, lax.rem(peer, block), across, peer).start())
+            probes[p, across] = help_share[p, lax.rem(c, block)]
+
     mix_slot(0)
+
+    @pl.when(helper)
+    def _():
+        help_modes.wait_recv()
+        when(jnp.logical_not(even), help_pass.start)
+        stack_modes(help_stack, help_own, 0)
+
+    help_slot(0)
     send_modes.wait_recv()
-    stack_modes(nxt.at[0], split)
+    stack_modes(stack, nxt, split)
     mix_slot(1)
+
+    @pl.when(helper)
+    def _():
+        help_next.wait_recv()
+        stack_modes(help_stack, help_nxt, split)
+
+    help_slot(1)
+    when(carry_west, west_turn.wait_recv, west_pass.start)
+    when(carry_east, east_turn.wait_recv, east_pass.start)
     to_south.wait_recv()
     north_west = remote(ext.at[:, first, low], ext.at[:, first, last], 5, {"col": west})
     north_east = remote(ext.at[:, first, high], ext.at[:, first, first], 6, {"col": east})
-    north_west.start()
-    north_east.start()
+    when(has_west, north_west.start)
+    when(has_east, north_east.start)
     to_north.wait_recv()
     south_west = remote(ext.at[:, last, low], ext.at[:, last, last], 7, {"col": west})
     south_east = remote(ext.at[:, last, high], ext.at[:, last, first], 8, {"col": east})
-    south_west.start()
-    south_east.start()
+    when(has_west, south_west.start)
+    when(has_east, south_east.start)
     for p in range(2, slots):
         mix_slot(p)
+        help_slot(p)
 
     repeat_t = where_bf16(iota((width, PAD), 1) == lax.div(iota((width, PAD), 0), strip))
     diagonal_t = lax.rem(iota((width, size), 0), strip) == lax.rem(iota((width, size), 1), strip)
@@ -176,10 +252,16 @@
     for load in loads[4:]:
         load.wait()
 
-    for copy in (to_west, to_east, north_west, north_east, south_west, south_east):
-        copy.wait_recv()
-    for copy in (to_north, to_south, to_west, to_east, north_west, north_east, south_west, south_east):
+    when(has_east, *(copy.wait_recv for copy in (to_west, north_west, south_west)))
+    when(has_west, *(copy.wait_recv for copy in (to_east, north_east, south_east)))
+    for copy in (to_north, to_south):
         copy.wait_send()
+    when(go_west, to_west.wait_send)
+    when(go_east, to_east.wait_send)
+    when(turn_west, west_turn.wait_send)
+    when(turn_east, east_turn.wait_send)
+    when(has_west, north_west.wait_send, south_west.wait_send)
+    when(has_east, north_east.wait_send, south_east.wait_send)
     for edge, box in (
         (r == 0, (slice(None), first, slice(None))),
         (r == rows - 1, (slice(None), last, slice(None))),
@@ -208,7 +290,8 @@
         got_terms[p, c] = terms[p, c]
 
     def position(p):
-        arrived(probes.at[p, others], probe_recv.at[p])
+        when(outer, lambda: arrived(probes.at[p, others], probe_recv.at[p]))
+        when(helper, lambda: arrived(probes.at[p, pl.ds(0, cols - 2)], probe_recv.at[p]))
         pr_re = probes[p, :, 0].reshape(size, size).astype(F32)
         pr_im = probes[p, :, 1].reshape(size, size).astype(F32)
         w_re = windows[p, 0].astype(F32)
@@ -240,28 +323,43 @@
 
     out_cols[0] = acc[:, :, first].astype(BF16)
     out_cols[1] = acc[:, :, last].astype(BF16)
-    cols_west = remote(out_cols.at[0], got_cols.at[1], 9, {"col": west})
-    cols_east = remote(out_cols.at[1], got_cols.at[0], 10, {"col": east})
-    cols_west.start()
-    cols_east.start()
+    top, bottom = pl.ds(0, size), pl.ds(size, size)
+    cols_west = [remote(out_cols.at[0, :, rows_of], got_cols.at[1, :, rows_of], i, {"col": west})
+                 for i, rows_of in ((9, top), (20, bottom))]
+    cols_east = [remote(out_cols.at[1, :, rows_of], got_cols.at[0, :, rows_of], i, {"col": east})
+                 for i, rows_of in ((10, top), (21, bottom))]
+    west_turn_out = remote(out_cols.at[0, :, top], carried_out.at[0], 22, {"col": c + side - 1})
+    east_turn_out = remote(out_cols.at[1, :, top], carried_out.at[1], 23, {"col": c - side + 1})
+    west_pass_out = remote(carried_out.at[0], got_cols.at[1, :, top], 9, {"col": c - side}, 24)
+    east_pass_out = remote(carried_out.at[1], got_cols.at[0, :, top], 10, {"col": c + side}, 25)
+    when(turn_west, west_turn_out.start)
+    when(turn_east, east_turn_out.start)
+    when(go_west, cols_west[0].start)
+    when(go_east, cols_east[0].start)
+    when(has_west, cols_west[1].start)
+    when(has_east, cols_east[1].start)
     send_terms(slots - 1)
 
-    def gather(p, half_of):
+    def gather(p, part_of):
         both = jnp.concatenate([got_terms[p, :, plane].reshape(size, size) for plane in range(2)], axis=1)
-        spot = pl.ds(half_of * split, split)
-        value = dot(kron_t[0, p, spot], both) + dot(kron_t[1, p, spot], both)
+        where = pl.ds(part_of * split, split)
+        value = dot(kron_t[0, p, where], both) + dot(kron_t[1, p, where], both)
         if p == 0:
-            sums[spot] = value
+            sums[where] = value
         else:
-            sums[spot] += value
-
-    for p in range(slots - 2):
+            sums[where] += value
+
+    arrived(got_terms.at[0, others], term_recv.at[0])
+    gather(0, 1)
+    when(carry_west, west_turn_out.wait_recv, west_pass_out.start)
+    when(carry_east, east_turn_out.wait_recv, east_pass_out.start)
+    for p in range(1, slots - 2):
         arrived(got_terms.at[p, others], term_recv.at[p])
         gather(p, 1)
 
-    cols_east.wait_recv()
+    when(has_west, *(copy.wait_recv for copy in cols_east))
     acc[:, :, low] += jnp.where(c == 0, 0.0, got_cols[0].astype(F32))
-    cols_west.wait_recv()
+    when(has_east, *(copy.wait_recv for copy in cols_west))
     acc[:, :, high] += jnp.where(c == cols - 1, 0.0, got_cols[1].astype(F32))
     out_rows[0] = acc[:, first, inner].astype(BF16)
     out_rows[1] = acc[:, last, inner].astype(BF16)
@@ -290,11 +388,25 @@
         own = sums[:split, pl.ds(plane * size, size)].reshape(num_modes, strip, size)
         mode_ref[0, :, plane] = own + got_sums[:, plane].astype(F32)
 
-    for copy in (send_modes, cols_west, cols_east, rows_north, rows_south, send_sums):
+    for copy in (send_modes, rows_north, rows_south, send_sums):
         copy.wait_send()
+    when(outer, help_modes.wait_send)
+    when(outer & even, help_next.wait_send)
+    when(helper & jnp.logical_not(even), help_pass.wait_send)
+    when(carry_west, west_pass.wait_send, west_pass_out.wait_send)
+    when(carry_east, east_pass.wait_send, east_pass_out.wait_send)
+    when(turn_west, west_turn_out.wait_send)
+    when(turn_east, east_turn_out.wait_send)
+    when(go_west, cols_west[0].wait_send)
+    when(go_east, cols_east[0].wait_send)
+    when(has_west, cols_west[1].wait_send)
+    when(has_east, cols_east[1].wait_send)
     arrived(mixes.at[others], mix_send)
     for p in range(slots):
-        arrived(share.at[p, others], probe_send.at[p])
+        near = pl.ds(0, block - 1)
+        arrived(share.at[p, near], probe_send.at[p])
+        when(helper, lambda p=p: arrived(share.at[p, pl.ds(0, block)], probe_send.at[p]))
+        when(helper, lambda p=p: arrived(help_share.at[p, near], probe_send.at[p]))
         arrived(terms.at[p, others], term_send.at[p])
 
 
@@ -334,6 +446,12 @@
             pltpu.VMEM(pieces, BF16),
             pltpu.VMEM(pieces, BF16),
             pltpu.VMEM((slots, 2, size, size), BF16),
+            pltpu.VMEM(modes.shape, BF16),
+            pltpu.VMEM(modes.shape, BF16),
+            pltpu.VMEM((width, full), BF16),
+            pltpu.VMEM((slots, cols // 2, 2, strip, size), BF16),
+            pltpu.VMEM((2, 2, size, half), BF16),
+            pltpu.VMEM((2, 2, size, half), BF16),
             pltpu.VMEM(pieces, BF16),
             pltpu.VMEM(pieces, BF16),
             pltpu.VMEM((2, full, full), F32),
@@ -345,8 +463,8 @@
             pltpu.VMEM((num_modes, 2, strip, size), BF16),
             pltpu.VMEM((num_modes, 2, strip, size), BF16),
             dma((len(args),)),
-            dma((14,)),
-            dma((14,)),
+            dma((26,)),
+            dma((26,)),
             dma,
             dma,
             dma((slots,)),

time: 98.5 us -> 89.7 us (0.911)
  the two profiles are of different devices: /device:TPU:64 before, /device:TPU:209 now
where the time goes in v3:
time: 89.7 us; the launch traced here: 89.5 us
  Pallas kernels  85.6 us (95%)
  local copies, waits for them, and re-layouts  2.67 us (3%)
  between operations  1.3 us (1%)
    pallas_call x1, Pallas kernels, local(): pl.pallas_call(functools.partial(kernel, (rows, cols, slots, num_modes, s...  85.6 us
    unnamed x4, local copies, waits for them, and re-layouts  2.67 us

profile of v3, /device:TPU:209, one launch (start us, length us, event | category | flops | bytes accessed | tf_op | source)
XLA Modules:
  0.0 89.5 jit_solution(6545028777195720084)
XLA Ops:
  1.3 85.6 %ptychography.1 = (f32[2,256,256]{2,1,0:T(8,128)}, f32[1,12,2,16,256]{4,3,2,1,0:T(8,128)}) custom-call(f32[2,256,256]{2,1,0:T(8,128)} %object_hbm.1, bf16[1,12,2,16,256]{4,3,2,1,0:T(8,128)(2,1)} %modes_hbm.1, f32[1,1,4,12]{3,2,1,0:T(4,128)} %coeffs_hbm.1, s32[1,1,2,4]{3,2,1,0:T(2,128)} %bitcast.1, s32[1,1,4]{2,1,0:T(1,128)} %region_hbm.1, ...), custom_call_target="tpu_custom_call" | custom-call | tf_op jit(solution)/shard_map/ptychography/pallas_call | solution.py:430
  86.9 0.0 copy-start
  86.9 1.9 %copy.14 = f32[2,256,256]{2,1,0:T(8,128)} copy(f32[2,256,256]{2,1,0:T(8,128)} %get-tuple-element.4) | data formatting | bytes 1048576
  88.8 0.0 copy-done
  88.8 0.7 copy.15
Async XLA Ops:
  86.9 1.9 %copy-start = (f32[1,12,2,16,256]{4,3,2,1,0:T(8,128)S(1)}, f32[1,12,2,16,256]{4,3,2,1,0:T(8,128)}, u32[]{:S(2)}) copy-start(f32[1,12,2,16,256]{4,3,2,1,0:T(8,128)} %get-tuple-element.5) | copy-start | bytes 1179652

commit v4 on v3

--- a/solution.py
+++ b/solution.py
@@ -46,8 +46,8 @@
     object_ref, modes_ref, coeffs_ref, offsets_ref, region_ref, counts_ref, inten, m_ref, mt_ref,
     ext, nxt, mixes, stack, kron, kron_t, share, probes, windows,
     help_own, help_nxt, help_stack, help_share, carried, carried_out,
-    terms, got_terms, acc, out_cols, got_cols, out_rows, got_rows, sums, out_sums, got_sums,
-    local_sem, pair_send, pair_recv, mix_send, mix_recv, probe_send, probe_recv, term_send, term_recv,
+    terms, got_terms, got_help, help_sums, out_help, in_help, acc, out_cols, got_cols, out_rows, got_rows, sums, out_sums, got_sums,
+    local_sem, pair_send, pair_recv, mix_send, mix_recv, probe_send, probe_recv, term_send, term_recv, help_recv,
 ):
     rows, cols, slots, num_modes, strip = dims
     size = cols * strip
@@ -117,7 +117,8 @@
     for peer in (north, south):
         pl.semaphore_signal(barrier, inc=1, device_id={"row": peer}, device_id_type=MESH)
 
-    pl.semaphore_signal(barrier, inc=1, device_id={"row": south, "col": across}, device_id_type=MESH)
+    for peer in (north, south):
+        pl.semaphore_signal(barrier, inc=1, device_id={"row": peer, "col": across}, device_id_type=MESH)
     pairs = [
         (coeffs_hbm, coeffs_ref), (region_hbm, region_ref), (modes_hbm, modes_ref), (object_hbm, object_ref),
         (offsets_hbm, offsets_ref), (counts_hbm, counts_ref), (inten_hbm, inten), (m_hbm, m_ref), (mt_hbm, mt_ref),
@@ -136,7 +137,7 @@
     for load in loads[2:4]:
         load.wait()
     ext[:, inner, inner] = object_ref[...].astype(BF16)
-    pl.semaphore_wait(barrier, cols + 2)
+    pl.semaphore_wait(barrier, cols + 3)
 
     everyone(lambda peer: scatter(mixes.at[c], mixes.at[c], mix_send, mix_recv, peer).start())
     send_modes = remote(modes_ref, nxt, 0, {"row": north})
@@ -249,6 +250,11 @@
             select = where_bf16(iota(sel_shape, 0) == lax.div(iota(sel_shape, 1), strip) * SLOT_ROWS + p)
             kron_t[i, p] = jnp.where(diagonal_t, dot(wide_t, select), 0.0).astype(BF16)
     acc[...] = jnp.zeros_like(acc)
+
+    @pl.when(outer)
+    def _():
+        got_terms[:, pl.ds((1 - group) * block, block)] = jnp.zeros((slots, block, 2, strip, size), BF16)
+
     for load in loads[4:]:
         load.wait()
 
@@ -284,10 +290,47 @@
             windows[p, plane] = dot(pick_rows, narrow).astype(BF16)
 
     def send_terms(p):
-        everyone(
-            lambda peer: scatter(terms.at[p, peer], got_terms.at[p, c], term_send.at[p], term_recv.at[p], peer).start()
-        )
+        def direct(peer):
+            scatter(terms.at[p, peer], got_terms.at[p, c], term_send.at[p], term_recv.at[p], peer).start()
+
+        def helped(k):
+            target = (3 - 3 * group) * side + lax.rem(c + k, side)
+            spot_of = got_help.at[p, lax.rem(c, block)]
+            scatter(terms.at[p, target], spot_of, term_send.at[p], help_recv.at[p], lax.rem(target + block, cols)).start()
+
+        def step(k, carry):
+            direct((2 - group) * side + lax.rem(c + k, side))
+            return carry
+
+        def help_step(k, carry):
+            helped(k)
+            return carry
+
+        lax.fori_loop(0, side, step, 0)
+        when(outer, lambda: helped(0))
+        lax.fori_loop(1, side, help_step, 0)
+        half_of(group, 1, direct)
         got_terms[p, c] = terms[p, c]
+
+        @pl.when(helper)
+        def _():
+            got_help[p, lax.rem(c, block)] = terms[p, across]
+
+    def terms_here(p):
+        when(outer, lambda: arrived(got_terms.at[p, pl.ds(0, block - 1)], term_recv.at[p]))
+        when(helper, lambda: arrived(got_terms.at[p, others], term_recv.at[p]))
+
+    def gather_help(p):
+        @pl.when(helper)
+        def _():
+            arrived(got_help.at[p, pl.ds(0, block - 1)], help_recv.at[p])
+            both = jnp.concatenate([got_help[p, :, part].reshape(half, size) for part in range(2)], axis=1)
+            lanes = pl.ds(pl.multiple_of(group * half, half), half)
+            value = dot(kron_t[0, p, :, lanes], both) + dot(kron_t[1, p, :, lanes], both)
+            if p == 0:
+                help_sums[...] = value
+            else:
+                help_sums[...] += value
 
     def position(p):
         when(outer, lambda: arrived(probes.at[p, others], probe_recv.at[p]))
@@ -349,13 +392,15 @@
         else:
             sums[where] += value
 
-    arrived(got_terms.at[0, others], term_recv.at[0])
+    terms_here(0)
     gather(0, 1)
+    gather_help(0)
     when(carry_west, west_turn_out.wait_recv, west_pass_out.start)
     when(carry_east, east_turn_out.wait_recv, east_pass_out.start)
     for p in range(1, slots - 2):
-        arrived(got_terms.at[p, others], term_recv.at[p])
+        terms_here(p)
         gather(p, 1)
+        gather_help(p)
 
     when(has_west, *(copy.wait_recv for copy in cols_east))
     acc[:, :, low] += jnp.where(c == 0, 0.0, got_cols[0].astype(F32))
@@ -369,7 +414,21 @@
     rows_south.start()
 
     for p in range(slots - 2, slots):
-        arrived(got_terms.at[p, others], term_recv.at[p])
+        gather_help(p)
+    help_back = remote(out_help.at[0], in_help.at[0], 26, {"row": r, "col": across})
+    help_down = remote(out_help.at[1], in_help.at[1], 27, {"row": south, "col": across})
+
+    @pl.when(helper)
+    def _():
+        for i in range(2):
+            for part in range(2):
+                value = help_sums[i * split : (i + 1) * split, pl.ds(part * size, size)].astype(BF16)
+                out_help[i, :, part] = value.reshape(num_modes, strip, size)
+        help_back.start()
+        help_down.start()
+
+    for p in range(slots - 2, slots):
+        terms_here(p)
         gather(p, 1)
     for plane in range(2):
         part = sums[split:, pl.ds(plane * size, size)].astype(BF16)
@@ -384,9 +443,13 @@
     rows_north.wait_recv()
     grad_ref[:, pl.ds(half, half), :] = acc[:, high, inner] + jnp.where(r == rows - 1, 0.0, got_rows[1].astype(F32))
     send_sums.wait_recv()
-    for plane in range(2):
-        own = sums[:split, pl.ds(plane * size, size)].reshape(num_modes, strip, size)
-        mode_ref[0, :, plane] = own + got_sums[:, plane].astype(F32)
+    when(outer, help_back.wait_recv, help_down.wait_recv)
+    for part in range(2):
+        own = sums[:split, pl.ds(part * size, size)].reshape(num_modes, strip, size)
+        extra = in_help[0, :, part].astype(F32) + in_help[1, :, part].astype(F32)
+        mode_ref[0, :, part] = own + got_sums[:, part].astype(F32) + jnp.where(outer, extra, 0.0)
+
+    when(helper, help_back.wait_send, help_down.wait_send)
 
     for copy in (send_modes, rows_north, rows_south, send_sums):
         copy.wait_send()
@@ -407,7 +470,8 @@
         arrived(share.at[p, near], probe_send.at[p])
         when(helper, lambda p=p: arrived(share.at[p, pl.ds(0, block)], probe_send.at[p]))
         when(helper, lambda p=p: arrived(help_share.at[p, near], probe_send.at[p]))
-        arrived(terms.at[p, others], term_send.at[p])
+        when(outer, lambda p=p: arrived(terms.at[p, others], term_send.at[p]))
+        when(helper, lambda p=p: arrived(terms.at[p, pl.ds(0, cols - 2)], term_send.at[p]))
 
 
 def local(object_field, modes, coeffs, offsets, region, counts, intensity):
@@ -454,6 +518,10 @@
             pltpu.VMEM((2, 2, size, half), BF16),
             pltpu.VMEM(pieces, BF16),
             pltpu.VMEM(pieces, BF16),
+            pltpu.VMEM((slots, cols // 2, 2, strip, size), BF16),
+            pltpu.VMEM((width, full), F32),
+            pltpu.VMEM((2, num_modes, 2, strip, size), BF16),
+            pltpu.VMEM((2, num_modes, 2, strip, size), BF16),
             pltpu.VMEM((2, full, full), F32),
             pltpu.VMEM((2, 2, full, half), BF16),
             pltpu.VMEM((2, 2, full, half), BF16),
@@ -463,10 +531,11 @@
             pltpu.VMEM((num_modes, 2, strip, size), BF16),
             pltpu.VMEM((num_modes, 2, strip, size), BF16),
             dma((len(args),)),
-            dma((26,)),
-            dma((26,)),
+            dma((28,)),
+            dma((28,)),
             dma,
             dma,
+            dma((slots,)),
             dma((slots,)),
             dma((slots,)),
             dma((slots,)),

time: 89.7 us -> 94 us (1.048)
  the two profiles are of different devices: /device:TPU:209 before, /device:TPU:64 now
where the time goes in v4:
time: 94 us; the launch traced here: 93.6 us
  Pallas kernels  89.7 us (95%)
  local copies, waits for them, and re-layouts  2.67 us (3%)
  between operations  1.3 us (1%)
    pallas_call x1, Pallas kernels, local(): pl.pallas_call(functools.partial(kernel, (rows, cols, slots, num_modes, s...  89.7 us
    unnamed x4, local copies, waits for them, and re-layouts  2.67 us

profile of v4, /device:TPU:64, one launch (start us, length us, event | category | flops | bytes accessed | tf_op | source)
XLA Modules:
  0.0 93.6 jit_solution(4535271137722634380)
XLA Ops:
  1.3 89.7 %ptychography.1 = (f32[2,256,256]{2,1,0:T(8,128)}, f32[1,12,2,16,256]{4,3,2,1,0:T(8,128)}) custom-call(f32[2,256,256]{2,1,0:T(8,128)} %object_hbm.1, bf16[1,12,2,16,256]{4,3,2,1,0:T(8,128)(2,1)} %modes_hbm.1, f32[1,1,4,12]{3,2,1,0:T(4,128)} %coeffs_hbm.1, s32[1,1,2,4]{3,2,1,0:T(2,128)} %bitcast.1, s32[1,1,4]{2,1,0:T(1,128)} %region_hbm.1, ...), custom_call_target="tpu_custom_call" | custom-call | tf_op jit(solution)/shard_map/ptychography/pallas_call | solution.py:494
  90.9 0.0 copy-start
  91.0 1.9 %copy.14 = f32[2,256,256]{2,1,0:T(8,128)} copy(f32[2,256,256]{2,1,0:T(8,128)} %get-tuple-element.4) | data formatting | bytes 1048576
  92.9 0.0 copy-done
  92.9 0.7 copy.15
Async XLA Ops:
  90.9 1.9 %copy-start = (f32[1,12,2,16,256]{4,3,2,1,0:T(8,128)S(1)}, f32[1,12,2,16,256]{4,3,2,1,0:T(8,128)}, u32[]{:S(2)}) copy-start(f32[1,12,2,16,256]{4,3,2,1,0:T(8,128)} %get-tuple-element.5) | copy-start | bytes 1179652

commit v5 on v3

--- a/solution.py
+++ b/solution.py
@@ -214,16 +214,6 @@
         stack_modes(help_stack, help_own, 0)
 
     help_slot(0)
-    send_modes.wait_recv()
-    stack_modes(stack, nxt, split)
-    mix_slot(1)
-
-    @pl.when(helper)
-    def _():
-        help_next.wait_recv()
-        stack_modes(help_stack, help_nxt, split)
-
-    help_slot(1)
     when(carry_west, west_turn.wait_recv, west_pass.start)
     when(carry_east, east_turn.wait_recv, east_pass.start)
     to_south.wait_recv()
@@ -236,6 +226,16 @@
     south_east = remote(ext.at[:, last, high], ext.at[:, last, first], 8, {"col": east})
     when(has_west, south_west.start)
     when(has_east, south_east.start)
+    send_modes.wait_recv()
+    stack_modes(stack, nxt, split)
+    mix_slot(1)
+
+    @pl.when(helper)
+    def _():
+        help_next.wait_recv()
+        stack_modes(help_stack, help_nxt, split)
+
+    help_slot(1)
     for p in range(2, slots):
         mix_slot(p)
         help_slot(p)
@@ -430,8 +430,8 @@
     return pl.pallas_call(
         functools.partial(kernel, (rows, cols, slots, num_modes, strip)),
         out_shape=(
-            jax.ShapeDtypeStruct((2, size, size), F32),
-            jax.ShapeDtypeStruct((1, num_modes, 2, strip, size), F32),
+            pltpu.VMEM((2, size, size), F32),
+            pltpu.VMEM((1, num_modes, 2, strip, size), F32),
         ),
         in_specs=[hbm] * len(args),
         out_specs=(vmem, vmem),

time: 89.7 us -> 86.2 us (0.961)
  the two profiles are of different devices: /device:TPU:209 before, /device:TPU:64 now
where the time goes in v5:
time: 86.2 us; the launch traced here: 84.7 us
  Pallas kernels  81.9 us (95%)
  local copies, waits for them, and re-layouts  1.54 us (2%)
  between operations  1.29 us (1%)
    pallas_call x1, Pallas kernels, local(): pl.pallas_call(functools.partial(kernel, (rows, cols, slots, num_modes, s...  81.9 us

profile of v5, /device:TPU:64, one launch (start us, length us, event | category | flops | bytes accessed | tf_op | source)
XLA Modules:
  0.0 84.7 jit_solution(3052546655555365147)
XLA Ops:
  1.3 81.9 %ptychography.1 = (f32[2,256,256]{2,1,0:T(8,128)S(1)}, f32[1,12,2,16,256]{4,3,2,1,0:T(8,128)S(1)}) custom-call(f32[2,256,256]{2,1,0:T(8,128)} %object_hbm.1, bf16[1,12,2,16,256]{4,3,2,1,0:T(8,128)(2,1)} %modes_hbm.1, f32[1,1,4,12]{3,2,1,0:T(4,128)} %coeffs_hbm.1, s32[1,1,2,4]{3,2,1,0:T(2,128)} %bitcast.1, s32[1,1,4]{2,1,0:T(1,128)} %region_hbm.1, ...), custom_call_target="tpu_custom_call" | custom-call | tf_op jit(solution)/shard_map/ptychography/pallas_call | solution.py:430
  83.2 0.8 copy.13
  84.0 0.7 copy.14

commit v6 on v5

--- a/solution.py
+++ b/solution.py
@@ -75,6 +75,9 @@
     turn_east = (spot == side - 1) & has_east
     carry_west = (spot == side - 1) & (plane > 0)
     carry_east = (spot == 0) & (plane < 3)
+    pass_west = (spot > 0) & (plane > 0)
+    pass_east = (spot < side - 1) & (plane < 3)
+    west_end, east_end = plane * side - 1, (plane + 1) * side
 
     def remote(src, dst, index, device, sender=None):
         return pltpu.make_async_remote_copy(
@@ -323,21 +326,23 @@
 
     out_cols[0] = acc[:, :, first].astype(BF16)
     out_cols[1] = acc[:, :, last].astype(BF16)
-    top, bottom = pl.ds(0, size), pl.ds(size, size)
-    cols_west = [remote(out_cols.at[0, :, rows_of], got_cols.at[1, :, rows_of], i, {"col": west})
-                 for i, rows_of in ((9, top), (20, bottom))]
-    cols_east = [remote(out_cols.at[1, :, rows_of], got_cols.at[0, :, rows_of], i, {"col": east})
-                 for i, rows_of in ((10, top), (21, bottom))]
-    west_turn_out = remote(out_cols.at[0, :, top], carried_out.at[0], 22, {"col": c + side - 1})
-    east_turn_out = remote(out_cols.at[1, :, top], carried_out.at[1], 23, {"col": c - side + 1})
-    west_pass_out = remote(carried_out.at[0], got_cols.at[1, :, top], 9, {"col": c - side}, 24)
-    east_pass_out = remote(carried_out.at[1], got_cols.at[0, :, top], 10, {"col": c + side}, 25)
-    when(turn_west, west_turn_out.start)
-    when(turn_east, east_turn_out.start)
-    when(go_west, cols_west[0].start)
-    when(go_east, cols_east[0].start)
-    when(has_west, cols_west[1].start)
-    when(has_east, cols_east[1].start)
+    quarter = full // 4
+
+    def piece(buffer, side_of, i):
+        return buffer.at[side_of, :, pl.ds(pl.multiple_of(i * quarter, quarter), quarter)]
+
+    cols_west = remote(out_cols.at[0], got_cols.at[1], 9, {"col": west})
+    cols_east = remote(out_cols.at[1], got_cols.at[0], 10, {"col": east})
+    west_parts = [remote(piece(out_cols, 0, i), piece(got_cols, 1, i), 26 + i, {"col": west}) for i in range(4)]
+    east_parts = [remote(piece(out_cols, 1, i), piece(got_cols, 0, i), 30 + i, {"col": east}) for i in range(4)]
+    west_turns = [remote(piece(out_cols, 0, i), carried_out.at[0], 22, {"col": c + i}, 34 + i) for i in range(1, 4)]
+    east_turns = [remote(piece(out_cols, 1, i), carried_out.at[1], 23, {"col": c - 3 + i}, 38 + i) for i in range(3)]
+    west_pass_out = remote(carried_out.at[0], piece(got_cols, 1, spot), 26 + spot, {"col": west_end}, 24)
+    east_pass_out = remote(carried_out.at[1], piece(got_cols, 0, spot), 30 + spot, {"col": east_end}, 25)
+    when(turn_west, *(copy.start for copy in west_turns), west_parts[0].start)
+    when(turn_east, *(copy.start for copy in east_turns), east_parts[3].start)
+    when(go_west, cols_west.start)
+    when(go_east, cols_east.start)
     send_terms(slots - 1)
 
     def gather(p, part_of):
@@ -351,15 +356,17 @@
 
     arrived(got_terms.at[0, others], term_recv.at[0])
     gather(0, 1)
-    when(carry_west, west_turn_out.wait_recv, west_pass_out.start)
-    when(carry_east, east_turn_out.wait_recv, east_pass_out.start)
+    when(pass_west, west_turns[0].wait_recv, west_pass_out.start)
+    when(pass_east, east_turns[0].wait_recv, east_pass_out.start)
     for p in range(1, slots - 2):
         arrived(got_terms.at[p, others], term_recv.at[p])
         gather(p, 1)
 
-    when(has_west, *(copy.wait_recv for copy in cols_east))
+    when(go_west, cols_east.wait_recv)
+    when(turn_west, *(copy.wait_recv for copy in east_parts))
     acc[:, :, low] += jnp.where(c == 0, 0.0, got_cols[0].astype(F32))
-    when(has_east, *(copy.wait_recv for copy in cols_west))
+    when(go_east, cols_west.wait_recv)
+    when(turn_east, *(copy.wait_recv for copy in west_parts))
     acc[:, :, high] += jnp.where(c == cols - 1, 0.0, got_cols[1].astype(F32))
     out_rows[0] = acc[:, first, inner].astype(BF16)
     out_rows[1] = acc[:, last, inner].astype(BF16)
@@ -393,14 +400,14 @@
     when(outer, help_modes.wait_send)
     when(outer & even, help_next.wait_send)
     when(helper & jnp.logical_not(even), help_pass.wait_send)
-    when(carry_west, west_pass.wait_send, west_pass_out.wait_send)
-    when(carry_east, east_pass.wait_send, east_pass_out.wait_send)
-    when(turn_west, west_turn_out.wait_send)
-    when(turn_east, east_turn_out.wait_send)
-    when(go_west, cols_west[0].wait_send)
-    when(go_east, cols_east[0].wait_send)
-    when(has_west, cols_west[1].wait_send)
-    when(has_east, cols_east[1].wait_send)
+    when(carry_west, west_pass.wait_send)
+    when(carry_east, east_pass.wait_send)
+    when(pass_west, west_pass_out.wait_send)
+    when(pass_east, east_pass_out.wait_send)
+    when(turn_west, *(copy.wait_send for copy in west_turns), west_parts[0].wait_send)
+    when(turn_east, *(copy.wait_send for copy in east_turns), east_parts[3].wait_send)
+    when(go_west, cols_west.wait_send)
+    when(go_east, cols_east.wait_send)
     arrived(mixes.at[others], mix_send)
     for p in range(slots):
         near = pl.ds(0, block - 1)
@@ -451,7 +458,7 @@
             pltpu.VMEM((width, full), BF16),
             pltpu.VMEM((slots, cols // 2, 2, strip, size), BF16),
             pltpu.VMEM((2, 2, size, half), BF16),
-            pltpu.VMEM((2, 2, size, half), BF16),
+            pltpu.VMEM((2, 2, full // 4, half), BF16),
             pltpu.VMEM(pieces, BF16),
             pltpu.VMEM(pieces, BF16),
             pltpu.VMEM((2, full, full), F32),
@@ -463,8 +470,8 @@
             pltpu.VMEM((num_modes, 2, strip, size), BF16),
             pltpu.VMEM((num_modes, 2, strip, size), BF16),
             dma((len(args),)),
-            dma((26,)),
-            dma((26,)),
+            dma((42,)),
+            dma((42,)),
             dma,
             dma,
             dma((slots,)),

time: 86.2 us -> 84.7 us (0.983)
  the two profiles are of different devices: /device:TPU:64 before, /device:TPU:4 now
where the time goes in v6:
time: 84.7 us; the launch traced here: 84.5 us
  Pallas kernels  81.7 us (96%)
  local copies, waits for them, and re-layouts  1.54 us (2%)
  between operations  1.29 us (2%)
    pallas_call x1, Pallas kernels, local(): pl.pallas_call(functools.partial(kernel, (rows, cols, slots, num_modes, s...  81.7 us

profile of v6, /device:TPU:4, one launch (start us, length us, event | category | flops | bytes accessed | tf_op | source)
XLA Modules:
  0.0 84.5 jit_solution(12309385685056721980)
XLA Ops:
  1.3 81.7 %ptychography.1 = (f32[2,256,256]{2,1,0:T(8,128)S(1)}, f32[1,12,2,16,256]{4,3,2,1,0:T(8,128)S(1)}) custom-call(f32[2,256,256]{2,1,0:T(8,128)} %object_hbm.1, bf16[1,12,2,16,256]{4,3,2,1,0:T(8,128)(2,1)} %modes_hbm.1, f32[1,1,4,12]{3,2,1,0:T(4,128)} %coeffs_hbm.1, s32[1,1,2,4]{3,2,1,0:T(2,128)} %bitcast.1, s32[1,1,4]{2,1,0:T(1,128)} %region_hbm.1, ...), custom_call_target="tpu_custom_call" | custom-call | tf_op jit(solution)/shard_map/ptychography/pallas_call | solution.py:437
  83.0 0.8 copy.13
  83.8 0.7 copy.14

commit v7 on v6

--- a/solution.py
+++ b/solution.py
@@ -193,8 +193,8 @@
         for part in range(2):
             value = both[:, part * size : (part + 1) * size].astype(BF16)
             share[p, :, part] = value.reshape(cols, strip, size)
+        when(helper, lambda: half_of(1 - group, 0, lambda peer: probe_copy(share, p, peer, c, peer).start()))
         half_of(group, 1, lambda peer: probe_copy(share, p, peer, c, peer).start())
-        when(helper, lambda: half_of(1 - group, 0, lambda peer: probe_copy(share, p, peer, c, peer).start()))
         probes[p, c] = share[p, c]
 
     def help_slot(p):

time: 84.7 us -> 84.5 us (level)
  the two profiles are of different devices: /device:TPU:4 before, /device:TPU:64 now
where the time goes in v7:
time: 84.5 us; the launch traced here: 83.5 us
  Pallas kernels  80.7 us (96%)
  local copies, waits for them, and re-layouts  1.54 us (2%)
  between operations  1.29 us (2%)
    pallas_call x1, Pallas kernels, local(): pl.pallas_call(functools.partial(kernel, (rows, cols, slots, num_modes, s...  80.7 us

profile of v7, /device:TPU:64, one launch (start us, length us, event | category | flops | bytes accessed | tf_op | source)
XLA Modules:
  0.0 83.5 jit_solution(19089488322675904)
XLA Ops:
  1.3 80.7 %ptychography.1 = (f32[2,256,256]{2,1,0:T(8,128)S(1)}, f32[1,12,2,16,256]{4,3,2,1,0:T(8,128)S(1)}) custom-call(f32[2,256,256]{2,1,0:T(8,128)} %object_hbm.1, bf16[1,12,2,16,256]{4,3,2,1,0:T(8,128)(2,1)} %modes_hbm.1, f32[1,1,4,12]{3,2,1,0:T(4,128)} %coeffs_hbm.1, s32[1,1,2,4]{3,2,1,0:T(2,128)} %bitcast.1, s32[1,1,4]{2,1,0:T(1,128)} %region_hbm.1, ...), custom_call_target="tpu_custom_call" | custom-call | tf_op jit(solution)/shard_map/ptychography/pallas_call | solution.py:437
  82.0 0.8 copy.13
  82.8 0.7 copy.14
